TPU v7x, 256 devices: a whole 4x4x8 slice. The times are simulated.
256 devices in a mesh: member: 16 (over z, y_hi), lat: 4 (over x), lon: 4 (over y_lo, core).
Axes of the slice: x: 4, y: 4 (y_hi: 2, y_lo: 2; y = y_hi * 2 + y_lo), z: 8, core: 2. Of those that a mesh axis runs over, the one named last changes fastest.
Arguments:
- ensemble: bfloat16 [32, 16, 64, 256], P('member', 'lat', 'lon'), may hold values from -12 to 12
- norm_gain: float32 [256], replicated, may hold values from 0.5 to 1.5
- project_weight: bfloat16 [256, 768], replicated, may hold values from -0.375 to 0.375
- output_weight: bfloat16 [256, 256], replicated, may hold values from -0.375 to 0.375
- conv_kernel: bfloat16 [3, 3, 256, 256], replicated, may hold values from -0.125 to 0.125
- cotangent: bfloat16 [32, 16, 64, 256], P('member', 'lat', 'lon'), may hold values from -6 to 6
Outputs:
- result: bfloat16 [32, 16, 64, 256], P('member', 'lat', 'lon')
- grad_ensemble: bfloat16 [32, 16, 64, 256], P('member', 'lat', 'lon')
All inputs are finite; a program needn't handle non-finite values.
Results may differ from a plain program's by a relative error of at most 0.018.
Values may be sent and summed in bfloat16 or wider, within the bound.
A program may use at most 64 MiB of HBM per device.

v0:
```python
import math

import jax
import jax.numpy as jnp
from jax import lax
from jax.sharding import PartitionSpec as P

HEAD_COUNT = 8


FLOOR = 0.5
EPSILON = 1e-06


def padded_2(block, sides, width, periodic):
    for axis, dim in sides:
        count = lax.axis_size(axis)
        forward = [(i, i + 1) for i in range(count - 1)]
        if periodic:
            forward.append((count - 1, 0))
        backward = [(target, source) for source, target in forward]
        low = lax.ppermute(
            lax.slice_in_dim(block, block.shape[dim] - width, None, axis=dim), axis, forward
        )
        high = lax.ppermute(lax.slice_in_dim(block, 0, width, axis=dim), axis, backward)
        block = jnp.concatenate([low, block, high], axis=dim)
    return block


def row_norm(values, gain_vec):
    mean_sq = jnp.mean(values * values, axis=-1, keepdims=True)
    return values * lax.rsqrt(mean_sq + EPSILON) * gain_vec


def head_norm(values, head_count):
    shaped = values.reshape(values.shape[:-1] + (head_count, values.shape[-1] // head_count))
    mean_sq = jnp.mean(shaped * shaped, axis=-1, keepdims=True)
    return (shaped * lax.rsqrt(jnp.maximum(mean_sq, FLOOR))).reshape(values.shape)


def split_heads(values, head_count):
    return values.reshape(values.shape[:-1] + (head_count, values.shape[-1] // head_count))


def head_pullback(raw_rows, grad_rows):
    _, pullback = jax.vjp(lambda t: head_norm(t, HEAD_COUNT), raw_rows.astype(jnp.float32))
    return pullback(grad_rows)[0]


def pad_field(field_in):
    widened = padded_2(field_in, (("lon", 2),), 1, True)
    return padded_2(widened, (("lat", 1),), 1, False)


def conv_taps(padded, kernel, lat_n, lon_n, adjoint):
    running = None
    for row_off in range(3):
        for col_off in range(3):
            if adjoint:
                window = padded[
                    :, 2 - row_off : 2 - row_off + lat_n, 2 - col_off : 2 - col_off + lon_n
                ]
                summand = jnp.einsum(
                    "mabc,dc->mabd",
                    window,
                    kernel[row_off, col_off],
                    preferred_element_type=jnp.float32,
                )
            else:
                window = padded[:, row_off : row_off + lat_n, col_off : col_off + lon_n]
                summand = jnp.einsum(
                    "mabc,cd->mabd",
                    window,
                    kernel[row_off, col_off],
                    preferred_element_type=jnp.float32,
                )
            running = summand if running is None else running + summand
    return running


def per_device(ensemble, norm_gain, project_weight, output_weight, conv_kernel, cotangent):
    mem_dev, lat_dev, lon_dev, channels = ensemble.shape
    cell_count = lat_dev * lon_dev
    score_scale = 1.0 / math.sqrt(channels // HEAD_COUNT)
    inputs = ensemble.reshape(mem_dev, cell_count, channels).astype(jnp.float32)
    normed = row_norm(inputs, norm_gain).astype(jnp.bfloat16)
    query_raw = jnp.dot(
        normed, project_weight[:, :channels], preferred_element_type=jnp.float32
    ).astype(jnp.bfloat16)
    gathered = jnp.dot(
        lax.all_gather(normed, "member", axis=0, tiled=True),
        project_weight[:, channels:],
        preferred_element_type=jnp.float32,
    ).astype(jnp.bfloat16)
    own_rows = lax.dynamic_slice_in_dim(gathered, lax.axis_index("member") * mem_dev, mem_dev, 0)
    key_raw = own_rows[..., :channels]
    key_rows = head_norm(gathered[..., :channels].astype(jnp.float32), HEAD_COUNT).astype(
        jnp.bfloat16
    )
    value_rows = gathered[..., channels:]
    queries = head_norm(query_raw.astype(jnp.float32), HEAD_COUNT).astype(jnp.bfloat16)
    query_heads = split_heads(queries, HEAD_COUNT)
    key_heads = split_heads(key_rows, HEAD_COUNT)
    value_heads = split_heads(value_rows, HEAD_COUNT)
    scores = (
        jnp.einsum("mphd,nphd->mnhp", query_heads, key_heads, preferred_element_type=jnp.float32)
        * score_scale
    )
    expd = jnp.exp(scores)
    soft = expd / jnp.sum(expd, axis=1, keepdims=True)
    rounded = soft.astype(jnp.bfloat16)
    mixed_out = jnp.einsum(
        "mnhp,nphd->mphd", rounded, value_heads, preferred_element_type=jnp.float32
    )
    mixed_out = mixed_out.reshape(query_raw.shape).astype(jnp.bfloat16)
    updated = (
        inputs + jnp.dot(mixed_out, output_weight, preferred_element_type=jnp.float32)
    ).astype(jnp.bfloat16)
    field_up = updated.reshape(mem_dev, lat_dev, lon_dev, channels)
    result = field_up.astype(jnp.float32) + conv_taps(
        pad_field(field_up), conv_kernel, lat_dev, lon_dev, False
    )
    result = result.astype(jnp.bfloat16)
    grad_field = cotangent.astype(jnp.float32) + conv_taps(
        pad_field(cotangent), conv_kernel, lat_dev, lon_dev, True
    )
    grad_rows = grad_field.reshape(mem_dev, cell_count, channels)
    grad_mixed = jnp.einsum(
        "mpc,dc->mpd",
        grad_rows.astype(jnp.bfloat16),
        output_weight,
        preferred_element_type=jnp.float32,
    )
    grad_mixed = grad_mixed.astype(jnp.bfloat16)
    grad_heads = split_heads(grad_mixed, HEAD_COUNT)
    dprob = jnp.einsum(
        "mphd,nphd->mnhp", grad_heads, value_heads, preferred_element_type=jnp.float32
    )
    dscore = (soft * (dprob - jnp.sum(soft * dprob, axis=1, keepdims=True))).astype(jnp.bfloat16)
    query_grad = (
        jnp.einsum("mnhp,nphd->mphd", dscore, key_heads, preferred_element_type=jnp.float32)
        * score_scale
    )
    query_grad = query_grad.reshape(query_raw.shape)
    row_count = mem_dev * lax.axis_size("member")
    key_part = (
        jnp.einsum("mnhp,mphd->nphd", dscore, query_heads, preferred_element_type=jnp.float32)
        * score_scale
    )
    value_part = jnp.einsum(
        "mnhp,mphd->nphd", rounded, grad_heads, preferred_element_type=jnp.float32
    )
    summed = lax.psum_scatter(
        jnp.concatenate(
            [
                key_part.reshape(row_count, cell_count, channels),
                value_part.reshape(row_count, cell_count, channels),
            ],
            axis=-1,
        ).astype(jnp.bfloat16),
        "member",
        scatter_dimension=0,
        tiled=True,
    ).astype(jnp.float32)
    key_grad = summed[..., :channels]
    value_grad = summed[..., channels:]
    grad_query_raw = head_pullback(query_raw, query_grad)
    grad_key_raw = head_pullback(key_raw, key_grad)
    grad_proj = jnp.concatenate([grad_query_raw, grad_key_raw, value_grad], axis=-1).astype(
        jnp.bfloat16
    )
    grad_normed = jnp.einsum(
        "mpe,ce->mpc", grad_proj, project_weight, preferred_element_type=jnp.float32
    )
    _, pull_norm = jax.vjp(lambda t: row_norm(t, norm_gain), inputs)
    grad_inputs = pull_norm(grad_normed)[0]
    grad_ensemble = (
        (grad_rows + grad_inputs).astype(jnp.bfloat16).reshape(mem_dev, lat_dev, lon_dev, channels)
    )
    return (result, grad_ensemble)


def solution(mesh):
    in_specs = (
        P("member", "lat", "lon", None),
        P(),
        P(),
        P(),
        P(),
        P("member", "lat", "lon", None),
    )
    out_specs = (P("member", "lat", "lon", None), P("member", "lat", "lon", None))
    return jax.shard_map(
        per_device, mesh=mesh, in_specs=in_specs, out_specs=out_specs, check_vma=False
    )
```

profile of v0, /device:TPU:1, one launch (start us, length us, event | category | flops | bytes accessed | tf_op | source)
XLA Modules:
  0.0 408.8 jit_solution(2294606689336277992)
XLA Ops:
  8.1 2.8 collective-permute-start.4
  20.1 4.0 collective-permute-start.7
  28.8 62.1 %all-gather.2.cloned.1.call-done = bf16[32,64,256]{2,1,0:T(8,128)(2,1)} async-done(((bf16[2,64,256]{2,1,0:T(8,128)(2,1)}), bf16[32,64,256]{2,1,0:T(8,128)(2,1)}) %all-gather.2.cloned.1.call-update) | async-done | bytes 1048592 | tf_op jit(solution)/shard_map/all_gather | solution.py:91
  98.1 6.5 %copy.153 = bf16[32,64,8,32]{3,0,1,2:T(8,128)(2,1)} copy(bf16[32,64,8,32]{1,3,2,0:T(8,128)(2,1)S(1)} %bitcast.179) | data formatting | bytes 2097152 | tf_op jit(solution)/shard_map/reshape | solution.py:42
  104.6 5.3 %fusion.115 = f32[8,64,32,2]{2,3,1,0:T(2,128)} fusion(bf16[32,64,8,32]{3,0,1,2:T(8,128)(2,1)} %copy.153, bf16[2,64,8,32]{3,0,1,2:T(2,128)(2,1)} %copy.154), kind=kOutput, calls=%fused_computation.175 | convolution fusion | flops 2097152 | bytes 1245184 | tf_op jit(solution)/shard_map/mphd,nphd->mnhp/dot_general | solution.py:136
  111.9 3.8 copy.139
  115.7 3.1 bitcast_reduce_fusion
  121.0 3.8 copy.140
  124.8 3.2 fusion
  130.8 7.5 %copy.145 = bf16[32,64,8,32]{3,0,1,2:T(8,128)(2,1)} copy(bf16[32,64,8,32]{1,3,2,0:T(8,128)(2,1)} %bitcast.181) | data formatting | bytes 2097152 | tf_op jit(solution)/shard_map/reshape | solution.py:42
  138.3 5.3 %fusion.114 = f32[8,64,32,2]{2,3,1,0:T(2,128)} fusion(bf16[32,64,8,32]{3,0,1,2:T(8,128)(2,1)} %copy.145, bf16[2,64,8,32]{3,0,1,2:T(2,128)(2,1)} %copy.146), kind=kOutput, calls=%fused_computation.174 | convolution fusion | flops 2097152 | bytes 1245184 | tf_op jit(solution)/shard_map/mphd,nphd->mnhp/dot_general | solution.py:106
  151.3 4.5 %multiply_convert_fusion = bf16[64,8,32,32]{3,2,1,0:T(8,128)(2,1)} fusion(bf16[2,64,8,32]{3,0,2,1:T(2,128)(2,1)} %copy.161, bf16[2,32,8,64]{1,0,2,3:T(2,128)(2,1)} %copy.157), kind=kOutput, calls=%fused_computation | convolution fusion | flops 3145728 | bytes 1179648 | tf_op jit(solution)/shard_map/mnhp,mphd->nphd/dot_general | solution.py:147
  155.8 4.9 %copy.167 = bf16[32,64,256]{2,1,0:T(8,128)(2,1)} copy(bf16[32,64,256]{0,2,1:T(8,128)(2,1)} %bitcast.183) | data formatting | bytes 2097152 | tf_op jit(solution)/shard_map/reshape | solution.py:156
  162.6 4.3 %convolution_convert_fusion = bf16[64,8,32,32]{3,2,1,0:T(8,128)(2,1)} fusion(bf16[2,64,8,32]{3,0,2,1:T(2,128)(2,1)} %copy.164, bf16[2,32,8,64]{1,0,2,3:T(2,128)(2,1)} %copy.149), kind=kOutput, calls=%fused_computation.2 | convolution fusion | flops 2621440 | bytes 1179648 | tf_op jit(solution)/shard_map/mnhp,mphd->nphd/dot_general | solution.py:150
  166.9 4.9 %copy.168 = bf16[32,64,256]{2,1,0:T(8,128)(2,1)} copy(bf16[32,64,256]{0,2,1:T(8,128)(2,1)} %bitcast.184) | data formatting | bytes 2097152 | tf_op jit(solution)/shard_map/reshape | solution.py:157
  171.8 3.1 pad_maximum_fusion
  174.9 7.8 %copy.156 = bf16[32,64,8,32]{3,0,2,1:T(8,128)(2,1)} copy(bf16[32,64,8,32]{1,3,2,0:T(8,128)(2,1)} %bitcast.182) | data formatting | bytes 2097152 | tf_op jit(solution)/shard_map/reshape | solution.py:42
  182.7 6.8 %copy.148 = bf16[32,64,8,32]{3,0,2,1:T(8,128)(2,1)} copy(bf16[32,64,8,32]{1,3,2,0:T(8,128)(2,1)S(1)} %bitcast.180) | data formatting | bytes 2097152 | tf_op jit(solution)/shard_map/reshape | solution.py:42
  189.5 3.4 fusion.116
  193.9 3.4 fusion.1
  197.5 182.2 %reduce-scatter.2.cloned.1.call-done = bf16[2,64,512]{2,1,0:T(8,128)(2,1)} async-done(((bf16[32,64,512]{2,1,0:T(8,128)(2,1)}), bf16[2,64,512]{2,1,0:T(8,128)(2,1)}) %reduce-scatter.2.cloned.1.call-update) | async-done | bytes 131088 | tf_op jit(solution)/shard_map/reduce_scatter | solution.py:153
  382.9 6.3 %collective-permute-start = (bf16[2,4,1,256]{3,2,1,0:T(2,128)(2,1)S(1)}, bf16[2,4,1,256]{3,2,1,0:T(2,128)(2,1)S(1)}, u32[]{:S(2)}, u32[]{:S(2)}) collective-permute-start(bf16[2,4,1,256]{3,2,1,0:T(2,128)(2,1)S(1)} %get-tuple-element.16), channel_id=1, source_target_pairs={{0,1},{1,2},{2,3},{3,0},{4,5},{5,6},{6,7},{7,4},{8,9},{9,10},{10,1... | collective-permute-start | bytes 12296 | tf_op jit(solution)/shard_map/ppermute | solution.py:22
  392.3 3.2 collective-permute-start.2
  397.0 3.1 collective-permute-done.3
  (119 shorter events, 49.0 us)
Async XLA Ops:
  7.2 19.4 %copy-start = (bf16[256,256]{1,0:T(8,128)(2,1)S(1)}, bf16[256,256]{1,0:T(8,128)(2,1)}, u32[]{:S(2)}) copy-start(bf16[256,256]{1,0:T(8,128)(2,1)} %param.9) | copy-start | bytes 393220
  7.2 11.6 %copy-start.5 = (bf16[2,4,16,256]{3,2,1,0:T(8,128)(2,1)S(1)}, bf16[2,4,16,256]{3,2,1,0:T(8,128)(2,1)}, u32[]{:S(2)}) copy-start(bf16[2,4,16,256]{3,2,1,0:T(8,128)(2,1)} %param.11) | copy-start | bytes 196612
  7.2 16.9 %copy-start.2 = (bf16[3,3,256,256]{3,2,1,0:T(8,128)(2,1)S(1)}, bf16[3,3,256,256]{3,2,1,0:T(8,128)(2,1)}, u32[]{:S(2)}) copy-start(bf16[3,3,256,256]{3,2,1,0:T(8,128)(2,1)} %param.10) | copy-start | bytes 3538948
  7.2 83.7 %all-gather.2.cloned.1.call-start = ((), (), s32[]{:S(2)}) async-start(), calls=%async_computation.1 | async-start | bytes 1114112 | tf_op jit(solution)/shard_map/all_gather | solution.py:91
  8.1 10.7 %collective-permute-start.4 = (bf16[2,4,1,256]{3,2,1,0:T(2,128)(2,1)S(1)}, bf16[2,4,1,256]{3,2,1,0:T(2,128)(2,1)S(1)}, u32[]{:S(2)}, u32[]{:S(2)}) collective-permute-start(bf16[2,4,1,256]{3,2,1,0:T(2,128)(2,1)S(1)} %get-tuple-element.18), channel_id=1, source_target_pairs={{0,1},{1,2},{2,3},{3,0},{4,5},{5,6},{6,7},{7,4},{8,9},{9,10},{10,1... | collective-permute-start | bytes 12296 | tf_op jit(solution)/shard_map/ppermute | solution.py:22
  10.9 7.9 %collective-permute-start.5 = (bf16[2,4,1,256]{3,2,1,0:T(2,128)(2,1)S(1)}, bf16[2,4,1,256]{3,2,1,0:T(2,128)(2,1)S(1)}, u32[]{:S(2)}, u32[]{:S(2)}) collective-permute-start(bf16[2,4,1,256]{3,2,1,0:T(2,128)(2,1)S(1)} %get-tuple-element.19), channel_id=1, source_target_pairs={{1,0},{2,1},{3,2},{0,3},{5,4},{6,5},{7,6},{4,7},{9,8},{10,9},{11,1... | collective-permute-start | bytes 12296 | tf_op jit(solution)/shard_map/ppermute | solution.py:25
  14.2 365.6 %reduce-scatter.2.cloned.1.call-start = ((), (), s32[]{:S(2)}) async-start(), calls=%async_computation.2 | async-start | bytes 2228224 | tf_op jit(solution)/shard_map/reduce_scatter | solution.py:153
  16.6 9.3 %copy-start.3 = (f32[2,64,256]{1,2,0:T(8,128)}, f32[2,64,256]{1,2,0:T(8,128)S(1)}, u32[]{:S(2)}) copy-start(f32[2,64,256]{1,2,0:T(8,128)S(1)} %copy.142) | copy-start | bytes 393220
  18.8 5.5 %collective-permute-start.6 = (bf16[2,1,18,256]{3,2,1,0:T(8,128)(2,1)S(1)}, bf16[2,1,18,256]{3,2,1,0:T(8,128)(2,1)S(1)}, u32[]{:S(2)}, u32[]{:S(2)}) collective-permute-start(bf16[2,1,18,256]{3,2,1,0:T(8,128)(2,1)S(1)} %get-tuple-element.14), channel_id=1, source_target_pairs={{4,0},{8,4},{12,8},{5,1},{9,5},{13,9},{6,2},{10,6},{14,10},{7,3},{... | collective-permute-start | bytes 55304 | tf_op jit(solution)/shard_map/ppermute | solution.py:25
  20.1 4.9 %collective-permute-start.7 = (bf16[2,1,18,256]{3,2,1,0:T(8,128)(2,1)S(1)}, bf16[2,1,18,256]{3,2,1,0:T(8,128)(2,1)S(1)}, u32[]{:S(2)}, u32[]{:S(2)}) collective-permute-start(bf16[2,1,18,256]{3,2,1,0:T(8,128)(2,1)S(1)} %get-tuple-element.15), channel_id=1, source_target_pairs={{0,4},{4,8},{8,12},{1,5},{5,9},{9,13},{2,6},{6,10},{10,14},{3,7},{... | collective-permute-start | bytes 55304 | tf_op jit(solution)/shard_map/ppermute | solution.py:22
  25.5 65.4 %copy-start.8 = (bf16[256,768]{1,0:T(8,128)(2,1)S(1)}, bf16[256,768]{1,0:T(8,128)(2,1)}, u32[]{:S(2)}) copy-start(bf16[256,768]{1,0:T(8,128)(2,1)} %param.8) | copy-start | bytes 1179652
  92.8 1.7 copy-start.1
  189.5 3.8 copy-start.4
  192.9 1.0 copy-start.6
  197.3 185.0 %copy-start.7 = (bf16[2,4,16,256]{3,2,1,0:T(8,128)(2,1)S(1)}, bf16[2,4,16,256]{3,2,1,0:T(8,128)(2,1)}, u32[]{:S(2)}) copy-start(bf16[2,4,16,256]{3,2,1,0:T(8,128)(2,1)} %param.6) | copy-start | bytes 196612
  197.3 185.0 %copy-start.9 = (bf16[256,768]{1,0:T(8,128)(2,1)S(1)}, bf16[256,768]{1,0:T(8,128)(2,1)}, u32[]{:S(2)}) copy-start(bf16[256,768]{1,0:T(8,128)(2,1)} %param.8) | copy-start | bytes 1179652
  197.3 185.0 %copy-start.11 = (f32[256]{0:T(256)S(1)}, f32[256]{0:T(256)}, u32[]{:S(2)}) copy-start(f32[256]{0:T(256)} %param.7) | copy-start | bytes 3076
  379.8 1.6 copy-start.10
  379.8 2.5 slice-start
  382.9 7.2 %collective-permute-start = (bf16[2,4,1,256]{3,2,1,0:T(2,128)(2,1)S(1)}, bf16[2,4,1,256]{3,2,1,0:T(2,128)(2,1)S(1)}, u32[]{:S(2)}, u32[]{:S(2)}) collective-permute-start(bf16[2,4,1,256]{3,2,1,0:T(2,128)(2,1)S(1)} %get-tuple-element.16), channel_id=1, source_target_pairs={{0,1},{1,2},{2,3},{3,0},{4,5},{5,6},{6,7},{7,4},{8,9},{9,10},{10,1... | collective-permute-start | bytes 12296 | tf_op jit(solution)/shard_map/ppermute | solution.py:22
  389.2 3.1 collective-permute-start.1
  392.3 4.7 %collective-permute-start.2 = (bf16[2,1,18,256]{3,2,1,0:T(8,128)(2,1)S(1)}, bf16[2,1,18,256]{3,2,1,0:T(8,128)(2,1)S(1)}, u32[]{:S(2)}, u32[]{:S(2)}) collective-permute-start(bf16[2,1,18,256]{3,2,1,0:T(8,128)(2,1)S(1)} %get-tuple-element.10), channel_id=1, source_target_pairs={{0,4},{4,8},{8,12},{1,5},{5,9},{9,13},{2,6},{6,10},{10,14},{3,7},{... | collective-permute-start | bytes 55304 | tf_op jit(solution)/shard_map/ppermute | solution.py:22
  395.5 4.6 %collective-permute-start.3 = (bf16[2,1,18,256]{3,2,1,0:T(8,128)(2,1)S(1)}, bf16[2,1,18,256]{3,2,1,0:T(8,128)(2,1)S(1)}, u32[]{:S(2)}, u32[]{:S(2)}) collective-permute-start(bf16[2,1,18,256]{3,2,1,0:T(8,128)(2,1)S(1)} %get-tuple-element.11), channel_id=1, source_target_pairs={{4,0},{8,4},{12,8},{5,1},{9,5},{13,9},{6,2},{10,6},{14,10},{7,3},{... | collective-permute-start | bytes 55304 | tf_op jit(solution)/shard_map/ppermute | solution.py:25
Sparse Core Ops, SparseCore 0:
  14.3 76.5 all-gather.1
  175.0 204.7 reduce-scatter.1
where the time goes:
time: 410 us; the launch traced here: 409 us
  waiting for transfers between devices  250 us (61%)
  local copies, waits for them, and re-layouts  69.1 us (17%)
  matrix products  34.8 us (8%)
  other arithmetic  20.5 us (5%)
  starting transfers between devices  19.5 us (5%)
  between operations  14.7 us (4%)
    reduce_scatter x1, waiting for transfers between devices, per_device(): lax.psum_scatter(jnp.concatenate([key_part.reshape(row_count, cell_count,...  182 us
    all_gather x1, waiting for transfers between devices, per_device(): lax.all_gather(normed, 'member', axis=0, tiled=True)  62.1 us
    reshape x8, local copies, waits for them, and re-layouts, split_heads(): values.reshape(values.shape[:-1] + (head_count, values.shape[-1] // head_...  32.2 us
    ppermute x4, starting transfers between devices, padded_2(): lax.ppermute(lax.slice_in_dim(block, block.shape[dim] - width, None, axis...  16.2 us
  transfers between devices with their start and end apart: 10, of which 5 were waited for; matrix products, arithmetic and copies ran while one was open for 8% of the time, Pallas kernels for 0%

commit v1 on v0

v1 whole, which is shorter than its diff:
```python
import math

import jax
import jax.numpy as jnp
from jax import lax
from jax.sharding import PartitionSpec as P

HEADS = 8
FLOOR = 0.5
EPSILON = 1e-06
BF = jnp.bfloat16
F32 = jnp.float32


def mm(a, b, dims):
    return lax.dot_general(a, b, (dims, ((), ())), preferred_element_type=F32)


def nn(a, b):
    return mm(a, b, ((1,), (0,)))


def nt(a, b):
    return mm(a, b, ((1,), (1,)))


def tn(a, b):
    return mm(a, b, ((0,), (0,)))


def head_blocks(channels, members):
    width = channels // HEADS
    row = lax.broadcasted_iota(jnp.int32, (HEADS * members, channels), 0) // members
    col = lax.broadcasted_iota(jnp.int32, (HEADS * members, channels), 1) // width
    return row == col


def spread(rows, blocks):
    return jnp.concatenate([rows] * HEADS, axis=0) * blocks


def head_scale(raw, ones):
    width = raw.shape[1] // HEADS
    mean_sq = nn((raw * raw).astype(BF), ones) * (1.0 / width)
    factor = lax.rsqrt(jnp.maximum(mean_sq, FLOOR))
    live = jnp.where(mean_sq > FLOOR, 1.0, jnp.where(mean_sq == FLOOR, 0.5, 0.0))
    return factor, live


def cell_forward(x, gain, w_proj, w_out, ones, members):
    rows, channels = x.shape
    cells = rows // members
    scale = 1.0 / math.sqrt(channels // HEADS)
    inputs = x.astype(F32)
    inv = lax.rsqrt(jnp.mean(inputs * inputs, axis=-1, keepdims=True) + EPSILON)
    normed = (inputs * inv * gain).astype(BF)
    proj = nn(normed, w_proj).astype(BF)
    q_raw = proj[:, :channels].astype(F32)
    k_raw = proj[:, channels : 2 * channels].astype(F32)
    values = proj[:, 2 * channels :]
    q_fac, q_live = head_scale(q_raw, ones)
    k_fac, k_live = head_scale(k_raw, ones)
    queries = (q_raw * q_fac).astype(BF)
    keys = (k_raw * k_fac).astype(BF)
    part = [slice(c * members, (c + 1) * members) for c in range(cells)]
    k_bd = [spread(keys[s], ones) for s in part]
    v_bd = [spread(values[s], ones) for s in part]
    scores = jnp.concatenate([nt(queries[s], k) for s, k in zip(part, k_bd)], axis=0)
    expd = jnp.exp(scores * scale)
    soft = expd / nn(expd.astype(BF), ones)
    rounded = soft.astype(BF)
    mixed = jnp.concatenate([nn(rounded[s], v) for s, v in zip(part, v_bd)], axis=0).astype(BF)
    updated = (inputs + nn(mixed, w_out)).astype(BF)
    saved = (inputs, inv, q_raw, k_raw, q_fac, k_fac, q_live, k_live, queries, k_bd, v_bd, soft, rounded)
    return updated, saved


def head_pull(raw, factor, live, grad, ones):
    width = raw.shape[1] // HEADS
    inner = nn((raw * grad).astype(BF), ones) * (1.0 / width)
    return grad * factor - raw * (factor * factor * factor * live * inner)


def fold(full, ones, members):
    kept = full * ones.astype(F32)
    total = kept[:members]
    for h in range(1, HEADS):
        total = total + kept[h * members : (h + 1) * members]
    return total


def cell_backward(grad_field, saved, gain, w_proj, w_out, ones, members):
    inputs, inv, q_raw, k_raw, q_fac, k_fac, q_live, k_live, queries, k_bd, v_bd, soft, rounded = saved
    rows, channels = inputs.shape
    cells = rows // members
    scale = 1.0 / math.sqrt(channels // HEADS)
    part = [slice(c * members, (c + 1) * members) for c in range(cells)]
    grad_mixed = nt(grad_field, w_out).astype(BF)
    dprob = jnp.concatenate([nt(grad_mixed[s], v) for s, v in zip(part, v_bd)], axis=0)
    delta = nn((soft * dprob).astype(BF), ones)
    dscore = (soft * (dprob - delta)).astype(BF)
    q_grad = jnp.concatenate([nn(dscore[s], k) for s, k in zip(part, k_bd)], axis=0) * scale
    k_grad = jnp.concatenate([fold(tn(dscore[s], queries[s]), ones, members) for s in part], axis=0) * scale
    v_grad = jnp.concatenate([fold(tn(rounded[s], grad_mixed[s]), ones, members) for s in part], axis=0)
    gq = head_pull(q_raw, q_fac, q_live, q_grad, ones).astype(BF)
    gk = head_pull(k_raw, k_fac, k_live, k_grad, ones).astype(BF)
    gv = v_grad.astype(BF)
    grad_normed = (
        nt(gq, w_proj[:, :channels])
        + nt(gk, w_proj[:, channels : 2 * channels])
        + nt(gv, w_proj[:, 2 * channels :])
    )
    lifted = grad_normed * gain
    inner = jnp.mean(lifted * inputs, axis=-1, keepdims=True)
    return lifted * inv - inputs * (inv * inv * inv * inner)


def padded(block):
    for axis, dim, periodic in (("lon", 2, True), ("lat", 1, False)):
        count = lax.axis_size(axis)
        forward = [(i, i + 1) for i in range(count - 1)]
        if periodic:
            forward.append((count - 1, 0))
        backward = [(t, s) for s, t in forward]
        low = lax.ppermute(lax.slice_in_dim(block, block.shape[dim] - 1, None, axis=dim), axis, forward)
        high = lax.ppermute(lax.slice_in_dim(block, 0, 1, axis=dim), axis, backward)
        block = jnp.concatenate([low, block, high], axis=dim)
    return block


def conv_taps(field, kernel, adjoint):
    mem, lat, lon, channels = field.shape
    wide = padded(field)
    total = None
    for r in range(3):
        for c in range(3):
            i, j = (2 - r, 2 - c) if adjoint else (r, c)
            window = wide[:, i : i + lat, j : j + lon].reshape(mem * lat * lon, channels)
            term = nt(window, kernel[r, c]) if adjoint else nn(window, kernel[r, c])
            total = term if total is None else total + term
    return total


def to_cells(rows):
    mem, lat, lon, channels = rows.shape
    count = lax.axis_size("member")
    out = rows.reshape(mem, lat, count, lon // count, channels).transpose(2, 1, 3, 0, 4)
    out = lax.all_to_all(out, "member", 0, 0, tiled=True)
    return out.transpose(1, 2, 0, 3, 4).reshape(-1, channels)


def to_home(rows, shape):
    mem, lat, lon, channels = shape
    count = lax.axis_size("member")
    out = rows.reshape(lat, lon // count, count, mem, channels).transpose(2, 0, 1, 3, 4)
    out = lax.all_to_all(out, "member", 0, 0, tiled=True)
    return out.transpose(3, 1, 0, 2, 4).reshape(shape)


def per_device(ensemble, norm_gain, project_weight, output_weight, conv_kernel, cotangent):
    mem, lat, lon, channels = ensemble.shape
    members = mem * lax.axis_size("member")
    ones = head_blocks(channels, members).astype(BF)
    gain = norm_gain.reshape(1, channels)
    x = to_cells(ensemble)
    updated, saved = cell_forward(x, gain, project_weight, output_weight, ones, members)
    field = to_home(updated, ensemble.shape)
    grad_field = cotangent.astype(F32).reshape(-1, channels) + conv_taps(cotangent, conv_kernel, True)
    grad_cells = to_cells(grad_field.astype(BF).reshape(ensemble.shape))
    grad_inputs = cell_backward(grad_cells, saved, gain, project_weight, output_weight, ones, members)
    result = field.astype(F32).reshape(-1, channels) + conv_taps(field, conv_kernel, False)
    back = to_home(grad_inputs.astype(BF), ensemble.shape).astype(F32).reshape(-1, channels)
    return (
        result.astype(BF).reshape(ensemble.shape),
        (grad_field + back).astype(BF).reshape(ensemble.shape),
    )


def solution(mesh):
    field = P("member", "lat", "lon", None)
    return jax.shard_map(
        per_device,
        mesh=mesh,
        in_specs=(field, P(), P(), P(), P(), field),
        out_specs=(field, field),
        check_vma=False,
    )
```

time: 410 us -> 91.1 us (0.22)
  waiting for transfers between devices: 250 us -> 8.78 us
  local copies, waits for them, and re-layouts: 69.1 us -> 6.26 us
  starting transfers between devices: 19.5 us -> 52.6 us
  matrix products: 34.8 us -> 17 us
  other arithmetic: 20.5 us -> 4.03 us
  between operations: 14.7 us -> 1.66 us
    reduce_scatter x1 -> x0, waiting for transfers between devices: 182 us -> none  [per_device(): lax.psum_scatter(jnp.concatenate([key_part.reshape(row_count, cell_count,...]
    all_gather x1 -> x0, waiting for transfers between devices: 62.1 us -> none  [per_device(): lax.all_gather(normed, 'member', axis=0, tiled=True)]
    reshape x11 -> x5, local copies, waits for them, and re-layouts: 42.1 us -> 1.46 us  [the longest x4 1.43 us: to_home(): rows.reshape(lat, lon // count, count, mem, channels)]
    all_to_all x0 -> x4, starting transfers between devices: none -> 34.5 us  [the longest x2 19.1 us: to_cells(): out = lax.all_to_all(out, 'member', 0, 0, tiled=True)]
    dot_general x29 -> x52, matrix products: 34.8 us -> 17 us  [mm(): return lax.dot_general(a, b, (dims, ((), ())), preferred_element_type=F32)]
    mul x9 -> x0, local copies, waits for them, and re-layouts: 10.3 us -> none  [the longest x7 6.42 us: head_norm(): shaped * lax.rsqrt(jnp.maximum(mean_sq, FLOOR))]
    convert_element_type x7 -> x3, local copies, waits for them, and re-layouts: 7.17 us -> 0.21 us  [the longest x2 0.16 us: cell_forward(): inputs = x.astype(F32)]
    convert_element_type x6 -> x4, other arithmetic: 7.39 us -> 0.82 us  [the longest x1 0.65 us: per_device(): (grad_field + back).astype(BF).reshape(ensemble.shape)]
  transfers between devices with their start and end apart: 10 -> 12, of which waited for: 5 -> 5; matrix products, arithmetic and copies ran while one was open for 8% -> 26% of each run, Pallas kernels for 0% -> 0%
where the time goes in v1:
time: 91.1 us; the launch traced here: 90.3 us
  starting transfers between devices  52.6 us (58%)
  matrix products  17 us (19%)
  waiting for transfers between devices  8.78 us (10%)
  local copies, waits for them, and re-layouts  6.26 us (7%)
  other arithmetic  4.03 us (4%)
  between operations  1.66 us (2%)
    all_to_all x2, starting transfers between devices, to_cells(): out = lax.all_to_all(out, 'member', 0, 0, tiled=True)  19.1 us
    dot_general x52, matrix products, mm(): return lax.dot_general(a, b, (dims, ((), ())), preferred_element_type=F32)  17 us
    all_to_all x2, starting transfers between devices, to_home(): out = lax.all_to_all(out, 'member', 0, 0, tiled=True)  15.4 us
    ppermute x4, starting transfers between devices, padded(): lax.ppermute(lax.slice_in_dim(block, block.shape[dim] - 1, None, axis=dim...  14.9 us
    ppermute x4, waiting for transfers between devices, padded(): high = lax.ppermute(lax.slice_in_dim(block, 0, 1, axis=dim), axis, backward)  5.4 us
    ppermute x4, starting transfers between devices, padded(): high = lax.ppermute(lax.slice_in_dim(block, 0, 1, axis=dim), axis, backward)  3.2 us
    unnamed x68, local copies, waits for them, and re-layouts  2.49 us
    all_to_all x2, waiting for transfers between devices, to_cells(): out = lax.all_to_all(out, 'member', 0, 0, tiled=True)  2.49 us
  transfers between devices with their start and end apart: 12, of which 5 were waited for; matrix products, arithmetic and copies ran while one was open for 26% of the time, Pallas kernels for 0%

profile of v1, /device:TPU:1, one launch (start us, length us, event | category | flops | bytes accessed | tf_op | source)
XLA Modules:
  0.0 90.3 jit_solution(10237813114785976373)
XLA Ops:
  0.7 0.9 fusion.245
  1.6 2.8 %collective-permute-start.4 = (bf16[2,4,1,256]{3,2,1,0:T(2,128)(2,1)S(1)}, bf16[2,4,1,256]{3,2,1,0:T(2,128)(2,1)S(1)}, u32[]{:S(2)}, u32[]{:S(2)}) collective-permute-start(bf16[2,4,1,256]{3,2,1,0:T(2,128)(2,1)S(1)} %get-tuple-element.35), channel_id=1, source_target_pairs={{0,1},{1,2},{2,3},{3,0},{4,5},{5,6},{6,7},{7,4},{8,9},{9,10},{10,1... | collective-permute-start | bytes 12296 | tf_op jit(solution)/shard_map/ppermute | solution.py:125
  4.9 1.5 %copy.35 = bf16[2,4,16,256]{3,1,0,2:T(4,128)(2,1)} copy(bf16[2,4,16,256]{3,2,1,0:T(8,128)(2,1)} %param.6) | data formatting | bytes 131072 | tf_op args[0]
  6.4 10.0 %all-to-all-start = ((bf16[16,4,1,2,256]{4,1,3,2,0:T(4,128)(2,1)}), bf16[16,4,1,2,256]{4,1,3,2,0:T(4,128)(2,1)S(1)}, u32[]{:S(2)}, u32[]{:S(2)}) async-start(bf16[16,4,1,2,256]{4,1,3,2,0:T(4,128)(2,1)} %bitcast.123), calls=%async_computation | async-start | bytes 131072 | tf_op jit(solution)/shard_map/all_to_all | solution.py:148
  16.5 1.1 %fusion.41 = f32[128,256]{1,0:T(8,128)S(1)} fusion(bf16[128,256]{1,0:T(8,128)(2,1)} %bitcast.130, bf16[3,3,256,256]{3,2,1,0:T(8,128)(2,1)} %param.10), kind=kOutput, calls=%fused_computation.154 | convolution fusion | flops 16777216 | bytes 327680 | tf_op jit(solution)/shard_map/dot_general | solution.py:16
  17.6 0.8 pad_maximum_fusion.10
  18.4 1.3 %collective-permute-start.6 = (bf16[2,1,18,256]{3,2,1,0:T(8,128)(2,1)S(1)}, bf16[2,1,18,256]{3,2,1,0:T(8,128)(2,1)S(1)}, u32[]{:S(2)}, u32[]{:S(2)}) collective-permute-start(bf16[2,1,18,256]{3,2,1,0:T(8,128)(2,1)S(1)} %get-tuple-element.27), channel_id=1, source_target_pairs={{4,0},{8,4},{12,8},{5,1},{9,5},{13,9},{6,2},{10,6},{14,10},{7,3},{... | collective-permute-start | bytes 55304 | tf_op jit(solution)/shard_map/ppermute | solution.py:126
  19.7 4.0 %collective-permute-start.7 = (bf16[2,1,18,256]{3,2,1,0:T(8,128)(2,1)S(1)}, bf16[2,1,18,256]{3,2,1,0:T(8,128)(2,1)S(1)}, u32[]{:S(2)}, u32[]{:S(2)}) collective-permute-start(bf16[2,1,18,256]{3,2,1,0:T(8,128)(2,1)S(1)} %get-tuple-element.28), channel_id=1, source_target_pairs={{0,4},{4,8},{8,12},{1,5},{5,9},{9,13},{2,6},{6,10},{10,14},{3,7},{... | collective-permute-start | bytes 55304 | tf_op jit(solution)/shard_map/ppermute | solution.py:125
  23.7 1.0 %pad_maximum_fusion.4 = (bf16[2,4,16,256]{3,2,1,0:T(8,128)(2,1)S(1)}, bf16[2,4,16,256]{3,2,1,0:T(8,128)(2,1)S(1)}) fusion(bf16[2,4,16,256]{3,2,1,0:T(8,128)(2,1)} %param.11, bf16[2,4,1,256]{3,2,1,0:T(2,128)(2,1)S(1)} %collective-permute-done.4, bf16[2,4,1,256]{3,2,1,0:T(2,128)(2,1)S(1)} %collective-permute-done.5), kind=kLoop, calls=%fused_computation.230 | loop fusion | flops 262144 | bytes 204800 | tf_op jit(solution)/shard_map/concatenate | solution.py:127
  24.7 1.0 %pad_maximum_fusion.3 = (bf16[2,5,18,256]{3,2,1,0:T(8,128)(2,1)S(1)}, bf16[2,5,18,256]{3,2,1,0:T(8,128)(2,1)S(1)}) fusion(bf16[2,1,18,256]{3,2,1,0:T(8,128)(2,1)S(1)} %collective-permute-done.6, bf16[2,4,1,256]{3,2,1,0:T(2,128)(2,1)S(1)} %collective-permute-done.5, bf16[2,4,16,256]{3,2,1,0:T(8,128)(2,1)} %param.11, ...), kind=kLoop, calls=%fused_computation.198 | loop fusion | flops 737280 | bytes 294912 | tf_op jit(solution)/shard_map/concatenate | solution.py:127
  28.2 9.1 %all-to-all-start.2 = ((bf16[16,4,1,2,256]{4,3,1,2,0:T(2,128)(2,1)}), bf16[16,4,1,2,256]{4,3,1,2,0:T(2,128)(2,1)S(1)}, u32[]{:S(2)}, u32[]{:S(2)}) async-start(bf16[16,4,1,2,256]{4,3,1,2,0:T(2,128)(2,1)} %bitcast.121), calls=%async_computation.2 | async-start | bytes 131072 | tf_op jit(solution)/shard_map/all_to_all | solution.py:148
  38.6 1.0 %fusion.24 = (bf16[128,256]{1,0:T(8,128)(2,1)S(1)}, bf16[128,256]{1,0:T(8,128)(2,1)S(1)}, f32[128,256]{1,0:T(8,128)}) fusion(bf16[128,768]{1,0:T(8,128)(2,1)S(1)} %convolution_convert_fusion, f32[128,256]{1,0:T(8,128)S(1)} %convolution_multiply_fusion.10, s32[256]{0:T(256)S(1)} %get-tuple-element.59, s32[256]{0:T(256)S(1)} %get-tuple-element.60, ...), kind=kOutput, calls=%fused_computation.132 | convolution fusion | flops 17367040 | bytes 594944 | tf_op jit(solution)/shard_map/dot_general | solution.py:16
  41.2 1.0 %fusion.248 = (bf16[128,256]{1,0:T(8,128)(2,1)S(1)}, f32[128,256]{1,0:T(8,128)}) fusion(s32[256]{0:T(256)S(1)} %get-tuple-element.59, s32[256]{0:T(256)S(1)} %get-tuple-element.60, pred[256]{0:T(512)(128)(4,1)S(1)} %compare_and_fusion, f32[32,256]{1,0:T(8,128)S(1)} %fusion.154, f32[32,256]{1,0:T(8,128)S(1)} %fusion.152, f32[32,256]{1,0:T(8,128)S(1)} %fusion.150, ...), kind=kOutput, calls=%fused_computation.437 | convolution fusion | flops 17334272 | bytes 329984 | tf_op jit(solution)/shard_map/dot_general | solution.py:16
  44.3 2.5 %all-to-all-done.2 = bf16[16,4,1,2,256]{4,3,1,2,0:T(2,128)(2,1)S(1)} async-done(((bf16[16,4,1,2,256]{4,3,1,2,0:T(2,128)(2,1)}), bf16[16,4,1,2,256]{4,3,1,2,0:T(2,128)(2,1)S(1)}, u32[]{:S(2)}, u32[]{:S(2)}) %all-to-all-start.2) | async-done | bytes 65568 | tf_op jit(solution)/shard_map/all_to_all | solution.py:148
  46.8 6.6 %all-to-all-start.1 = ((bf16[16,4,1,2,256]{4,1,3,2,0:T(4,128)(2,1)}), bf16[16,4,1,2,256]{4,1,3,2,0:T(4,128)(2,1)S(1)}, u32[]{:S(2)}, u32[]{:S(2)}) async-start(bf16[16,4,1,2,256]{4,1,3,2,0:T(4,128)(2,1)} %bitcast.122), calls=%async_computation.1 | async-start | bytes 131072 | tf_op jit(solution)/shard_map/all_to_all | solution.py:156
  53.6 0.9 %convolution_multiply_fusion.3 = f32[256,256]{1,0:T(8,128)S(1)} fusion(bf16[128,256]{1,0:T(8,128)(2,1)S(1)} %convolution_convert_fusion.1, bf16[128,256]{1,0:T(8,128)(2,1)} %copy-done.5, s32[256]{0:T(256)S(1)} %get-tuple-element.59, s32[256]{0:T(256)S(1)} %get-tuple-element.60, pred[256]{0:T(512)(128)(4,1)S(1)} %compare_and_fusion), kind=kOutput, calls=%fused_computation.4 | convolution fusion | flops 4587520 | bytes 300032 | tf_op jit(solution)/shard_map/dot_general | solution.py:16
  54.6 0.9 %convolution_multiply_fusion.2 = f32[256,256]{1,0:T(8,128)S(1)} fusion(bf16[128,256]{1,0:T(8,128)(2,1)S(1)} %convolution_convert_fusion.1, bf16[128,256]{1,0:T(8,128)(2,1)} %copy-done.5, s32[256]{0:T(256)S(1)} %get-tuple-element.59, s32[256]{0:T(256)S(1)} %get-tuple-element.60, pred[256]{0:T(512)(128)(4,1)S(1)} %compare_and_fusion), kind=kOutput, calls=%fused_computation.3 | convolution fusion | flops 4587520 | bytes 300032 | tf_op jit(solution)/shard_map/dot_general | solution.py:16
  62.7 8.8 %all-to-all-start.3 = ((bf16[16,4,1,2,256]{4,3,1,2,0:T(2,128)(2,1)}), bf16[16,4,1,2,256]{4,3,1,2,0:T(2,128)(2,1)S(1)}, u32[]{:S(2)}, u32[]{:S(2)}) async-start(bf16[16,4,1,2,256]{4,3,1,2,0:T(2,128)(2,1)} %bitcast.120), calls=%async_computation.3 | async-start | bytes 131072 | tf_op jit(solution)/shard_map/all_to_all | solution.py:156
  71.6 4.2 %collective-permute-start = (bf16[2,4,1,256]{3,2,1,0:T(2,128)(2,1)S(1)}, bf16[2,4,1,256]{3,2,1,0:T(2,128)(2,1)S(1)}, u32[]{:S(2)}, u32[]{:S(2)}) collective-permute-start(bf16[2,4,1,256]{3,2,1,0:T(2,128)(2,1)S(1)} %get-tuple-element.41), channel_id=1, source_target_pairs={{0,1},{1,2},{2,3},{3,0},{4,5},{5,6},{6,7},{7,4},{8,9},{9,10},{10,1... | collective-permute-start | bytes 12296 | tf_op jit(solution)/shard_map/ppermute | solution.py:125
  76.6 2.6 %collective-permute-done.1 = bf16[2,4,1,256]{3,2,1,0:T(2,128)(2,1)S(1)} collective-permute-done((bf16[2,4,1,256]{3,2,1,0:T(2,128)(2,1)S(1)}, bf16[2,4,1,256]{3,2,1,0:T(2,128)(2,1)S(1)}, u32[]{:S(2)}, u32[]{:S(2)}) %collective-permute-start.1) | collective-permute-done | bytes 4128 | tf_op jit(solution)/shard_map/ppermute | solution.py:126
  79.2 3.9 %collective-permute-start.2 = (bf16[2,1,18,256]{3,2,1,0:T(8,128)(2,1)S(1)}, bf16[2,1,18,256]{3,2,1,0:T(8,128)(2,1)S(1)}, u32[]{:S(2)}, u32[]{:S(2)}) collective-permute-start(bf16[2,1,18,256]{3,2,1,0:T(8,128)(2,1)S(1)} %get-tuple-element.31), channel_id=1, source_target_pairs={{0,4},{4,8},{8,12},{1,5},{5,9},{9,13},{2,6},{6,10},{10,14},{3,7},{... | collective-permute-start | bytes 55304 | tf_op jit(solution)/shard_map/ppermute | solution.py:125
  83.2 1.3 %collective-permute-start.3 = (bf16[2,1,18,256]{3,2,1,0:T(8,128)(2,1)S(1)}, bf16[2,1,18,256]{3,2,1,0:T(8,128)(2,1)S(1)}, u32[]{:S(2)}, u32[]{:S(2)}) collective-permute-start(bf16[2,1,18,256]{3,2,1,0:T(8,128)(2,1)S(1)} %get-tuple-element.32), channel_id=1, source_target_pairs={{4,0},{8,4},{12,8},{5,1},{9,5},{13,9},{6,2},{10,6},{14,10},{7,3},{... | collective-permute-start | bytes 55304 | tf_op jit(solution)/shard_map/ppermute | solution.py:126
  85.3 2.8 %collective-permute-done.3 = bf16[2,1,18,256]{3,2,1,0:T(8,128)(2,1)S(1)} collective-permute-done((bf16[2,1,18,256]{3,2,1,0:T(8,128)(2,1)S(1)}, bf16[2,1,18,256]{3,2,1,0:T(8,128)(2,1)S(1)}, u32[]{:S(2)}, u32[]{:S(2)}) %collective-permute-start.3) | collective-permute-done | bytes 18464 | tf_op jit(solution)/shard_map/ppermute | solution.py:126
  89.5 0.8 fusion.17
  (169 shorter events, 17.9 us)
Async XLA Ops:
  0.6 42.7 %copy-start = (bf16[256,256]{1,0:T(8,128)(2,1)S(1)}, bf16[256,256]{1,0:T(8,128)(2,1)}, u32[]{:S(2)}) copy-start(bf16[256,256]{1,0:T(8,128)(2,1)} %param.9) | copy-start | bytes 393220
  0.6 25.2 %copy-start.1 = (bf16[3,3,256,256]{3,2,1,0:T(8,128)(2,1)S(1)}, bf16[3,3,256,256]{3,2,1,0:T(8,128)(2,1)}, u32[]{:S(2)}) copy-start(bf16[3,3,256,256]{3,2,1,0:T(8,128)(2,1)} %param.10) | copy-start | bytes 3538948
  1.6 16.1 %collective-permute-start.4 = (bf16[2,4,1,256]{3,2,1,0:T(2,128)(2,1)S(1)}, bf16[2,4,1,256]{3,2,1,0:T(2,128)(2,1)S(1)}, u32[]{:S(2)}, u32[]{:S(2)}) collective-permute-start(bf16[2,4,1,256]{3,2,1,0:T(2,128)(2,1)S(1)} %get-tuple-element.35), channel_id=1, source_target_pairs={{0,1},{1,2},{2,3},{3,0},{4,5},{5,6},{6,7},{7,4},{8,9},{9,10},{10,1... | collective-permute-start | bytes 12296 | tf_op jit(solution)/shard_map/ppermute | solution.py:125
  4.3 13.3 %collective-permute-start.5 = (bf16[2,4,1,256]{3,2,1,0:T(2,128)(2,1)S(1)}, bf16[2,4,1,256]{3,2,1,0:T(2,128)(2,1)S(1)}, u32[]{:S(2)}, u32[]{:S(2)}) collective-permute-start(bf16[2,4,1,256]{3,2,1,0:T(2,128)(2,1)S(1)} %get-tuple-element.36), channel_id=1, source_target_pairs={{1,0},{2,1},{3,2},{0,3},{5,4},{6,5},{7,6},{4,7},{9,8},{10,9},{11,1... | collective-permute-start | bytes 12296 | tf_op jit(solution)/shard_map/ppermute | solution.py:126
  6.4 21.8 %all-to-all-start = ((bf16[16,4,1,2,256]{4,1,3,2,0:T(4,128)(2,1)}), bf16[16,4,1,2,256]{4,1,3,2,0:T(4,128)(2,1)S(1)}, u32[]{:S(2)}, u32[]{:S(2)}) async-start(bf16[16,4,1,2,256]{4,1,3,2,0:T(4,128)(2,1)} %bitcast.123), calls=%async_computation | async-start | bytes 131072 | tf_op jit(solution)/shard_map/all_to_all | solution.py:148
  18.4 6.3 %collective-permute-start.6 = (bf16[2,1,18,256]{3,2,1,0:T(8,128)(2,1)S(1)}, bf16[2,1,18,256]{3,2,1,0:T(8,128)(2,1)S(1)}, u32[]{:S(2)}, u32[]{:S(2)}) collective-permute-start(bf16[2,1,18,256]{3,2,1,0:T(8,128)(2,1)S(1)} %get-tuple-element.27), channel_id=1, source_target_pairs={{4,0},{8,4},{12,8},{5,1},{9,5},{13,9},{6,2},{10,6},{14,10},{7,3},{... | collective-permute-start | bytes 55304 | tf_op jit(solution)/shard_map/ppermute | solution.py:126
  19.7 5.0 %collective-permute-start.7 = (bf16[2,1,18,256]{3,2,1,0:T(8,128)(2,1)S(1)}, bf16[2,1,18,256]{3,2,1,0:T(8,128)(2,1)S(1)}, u32[]{:S(2)}, u32[]{:S(2)}) collective-permute-start(bf16[2,1,18,256]{3,2,1,0:T(8,128)(2,1)S(1)} %get-tuple-element.28), channel_id=1, source_target_pairs={{0,4},{4,8},{8,12},{1,5},{5,9},{9,13},{2,6},{6,10},{10,14},{3,7},{... | collective-permute-start | bytes 55304 | tf_op jit(solution)/shard_map/ppermute | solution.py:125
  26.2 1.1 %copy-start.2 = (bf16[2,4,16,256]{3,2,1,0:T(8,128)(2,1)S(1)}, bf16[2,4,16,256]{3,2,1,0:T(8,128)(2,1)}, u32[]{:S(2)}) copy-start(bf16[2,4,16,256]{3,2,1,0:T(8,128)(2,1)} %param.11) | copy-start | bytes 196612
  27.0 10.9 %copy-start.3 = (bf16[256,768]{1,0:T(8,128)(2,1)S(1)}, bf16[256,768]{1,0:T(8,128)(2,1)}, u32[]{:S(2)}) copy-start(bf16[256,768]{1,0:T(8,128)(2,1)} %param.8) | copy-start | bytes 1179652
  27.0 10.9 %copy-start.4 = (f32[256]{0:T(256)S(1)}, f32[256]{0:T(256)}, u32[]{:S(2)}) copy-start(f32[256]{0:T(256)} %param.7) | copy-start | bytes 3076
  28.2 18.6 %all-to-all-start.2 = ((bf16[16,4,1,2,256]{4,3,1,2,0:T(2,128)(2,1)}), bf16[16,4,1,2,256]{4,3,1,2,0:T(2,128)(2,1)S(1)}, u32[]{:S(2)}, u32[]{:S(2)}) async-start(bf16[16,4,1,2,256]{4,3,1,2,0:T(2,128)(2,1)} %bitcast.121), calls=%async_computation.2 | async-start | bytes 131072 | tf_op jit(solution)/shard_map/all_to_all | solution.py:148
  38.6 1.5 %copy-start.7 = (f32[128,256]{1,0:T(8,128)}, f32[128,256]{1,0:T(8,128)S(1)}, u32[]{:S(2)}) copy-start(f32[128,256]{1,0:T(8,128)S(1)} %convolution_multiply_fusion.10) | copy-start | bytes 393220
  42.2 0.9 copy-start.5
  46.8 16.0 %all-to-all-start.1 = ((bf16[16,4,1,2,256]{4,1,3,2,0:T(4,128)(2,1)}), bf16[16,4,1,2,256]{4,1,3,2,0:T(4,128)(2,1)S(1)}, u32[]{:S(2)}, u32[]{:S(2)}) async-start(bf16[16,4,1,2,256]{4,1,3,2,0:T(4,128)(2,1)} %bitcast.122), calls=%async_computation.1 | async-start | bytes 131072 | tf_op jit(solution)/shard_map/all_to_all | solution.py:156
  53.4 2.1 %copy-start.6 = (bf16[128,256]{1,0:T(8,128)(2,1)S(1)}, bf16[128,256]{1,0:T(8,128)(2,1)}, u32[]{:S(2)}) copy-start(bf16[128,256]{1,0:T(8,128)(2,1)} %copy-done.5) | copy-start | bytes 196612
  56.0 1.2 %copy-start.10 = (f32[128,256]{1,0:T(8,128)S(1)}, f32[128,256]{1,0:T(8,128)}, u32[]{:S(2)}) copy-start(f32[128,256]{1,0:T(8,128)} %get-tuple-element.54) | copy-start | bytes 393220
  59.5 0.9 %copy-start.9 = (f32[128,256]{1,0:T(8,128)S(1)}, f32[128,256]{1,0:T(8,128)}, u32[]{:S(2)}) copy-start(f32[128,256]{1,0:T(8,128)} %get-tuple-element.52) | copy-start | bytes 393220
  59.7 1.2 %copy-start.8 = (f32[128,256]{1,0:T(8,128)S(1)}, f32[128,256]{1,0:T(8,128)}, u32[]{:S(2)}) copy-start(f32[128,256]{1,0:T(8,128)} %copy-done.7) | copy-start | bytes 393220
  62.7 21.8 %all-to-all-start.3 = ((bf16[16,4,1,2,256]{4,3,1,2,0:T(2,128)(2,1)}), bf16[16,4,1,2,256]{4,3,1,2,0:T(2,128)(2,1)S(1)}, u32[]{:S(2)}, u32[]{:S(2)}) async-start(bf16[16,4,1,2,256]{4,3,1,2,0:T(2,128)(2,1)} %bitcast.120), calls=%async_computation.3 | async-start | bytes 131072 | tf_op jit(solution)/shard_map/all_to_all | solution.py:156
  71.6 5.0 %collective-permute-start = (bf16[2,4,1,256]{3,2,1,0:T(2,128)(2,1)S(1)}, bf16[2,4,1,256]{3,2,1,0:T(2,128)(2,1)S(1)}, u32[]{:S(2)}, u32[]{:S(2)}) collective-permute-start(bf16[2,4,1,256]{3,2,1,0:T(2,128)(2,1)S(1)} %get-tuple-element.41), channel_id=1, source_target_pairs={{0,1},{1,2},{2,3},{3,0},{4,5},{5,6},{6,7},{7,4},{8,9},{9,10},{10,1... | collective-permute-start | bytes 12296 | tf_op jit(solution)/shard_map/ppermute | solution.py:125
  75.8 3.4 %collective-permute-start.1 = (bf16[2,4,1,256]{3,2,1,0:T(2,128)(2,1)S(1)}, bf16[2,4,1,256]{3,2,1,0:T(2,128)(2,1)S(1)}, u32[]{:S(2)}, u32[]{:S(2)}) collective-permute-start(bf16[2,4,1,256]{3,2,1,0:T(2,128)(2,1)S(1)} %get-tuple-element.42), channel_id=1, source_target_pairs={{1,0},{2,1},{3,2},{0,3},{5,4},{6,5},{7,6},{4,7},{9,8},{10,9},{11,1... | collective-permute-start | bytes 12296 | tf_op jit(solution)/shard_map/ppermute | solution.py:126
  79.2 6.1 %collective-permute-start.2 = (bf16[2,1,18,256]{3,2,1,0:T(8,128)(2,1)S(1)}, bf16[2,1,18,256]{3,2,1,0:T(8,128)(2,1)S(1)}, u32[]{:S(2)}, u32[]{:S(2)}) collective-permute-start(bf16[2,1,18,256]{3,2,1,0:T(8,128)(2,1)S(1)} %get-tuple-element.31), channel_id=1, source_target_pairs={{0,4},{4,8},{8,12},{1,5},{5,9},{9,13},{2,6},{6,10},{10,14},{3,7},{... | collective-permute-start | bytes 55304 | tf_op jit(solution)/shard_map/ppermute | solution.py:125
  83.2 4.9 %collective-permute-start.3 = (bf16[2,1,18,256]{3,2,1,0:T(8,128)(2,1)S(1)}, bf16[2,1,18,256]{3,2,1,0:T(8,128)(2,1)S(1)}, u32[]{:S(2)}, u32[]{:S(2)}) collective-permute-start(bf16[2,1,18,256]{3,2,1,0:T(8,128)(2,1)S(1)} %get-tuple-element.32), channel_id=1, source_target_pairs={{4,0},{8,4},{12,8},{5,1},{9,5},{13,9},{6,2},{10,6},{14,10},{7,3},{... | collective-permute-start | bytes 55304 | tf_op jit(solution)/shard_map/ppermute | solution.py:126

commit v2 on v1

--- a/solution.py
+++ b/solution.py
@@ -1,8 +1,11 @@
+import functools
 import math
 
 import jax
 import jax.numpy as jnp
 from jax import lax
+from jax.experimental import pallas as pl
+from jax.experimental.pallas import tpu as pltpu
 from jax.sharding import PartitionSpec as P
 
 HEADS = 8
@@ -115,64 +118,350 @@
     return lifted * inv - inputs * (inv * inv * inv * inner)
 
 
-def padded(block):
-    for axis, dim, periodic in (("lon", 2, True), ("lat", 1, False)):
-        count = lax.axis_size(axis)
-        forward = [(i, i + 1) for i in range(count - 1)]
-        if periodic:
-            forward.append((count - 1, 0))
-        backward = [(t, s) for s, t in forward]
-        low = lax.ppermute(lax.slice_in_dim(block, block.shape[dim] - 1, None, axis=dim), axis, forward)
-        high = lax.ppermute(lax.slice_in_dim(block, 0, 1, axis=dim), axis, backward)
-        block = jnp.concatenate([low, block, high], axis=dim)
-    return block
-
-
-def conv_taps(field, kernel, adjoint):
-    mem, lat, lon, channels = field.shape
-    wide = padded(field)
-    total = None
-    for r in range(3):
+def iota(shape, dim):
+    return lax.broadcasted_iota(jnp.int32, shape, dim)
+
+
+def one_hot(shape, source):
+    return jnp.where(iota(shape, 1) == source(iota(shape, 0)), 1.0, 0.0).astype(BF)
+
+
+def pack(rows, peers):
+    half = rows.shape[1] // 2
+    per = rows.shape[0] // peers
+    low = rows[:, :half].reshape(peers, per, half)
+    high = rows[:, half:].reshape(peers, per, half)
+    return jnp.concatenate([low, high], axis=1).astype(BF)
+
+
+def unpack(chunks):
+    peers, double, half = chunks.shape
+    wide = chunks.astype(F32)
+    low = wide[:, : double // 2].reshape(peers * double // 2, half)
+    high = wide[:, double // 2 :].reshape(peers * double // 2, half)
+    return jnp.concatenate([low, high], axis=1).astype(BF)
+
+
+X, G, U, B = range(4)
+
+
+def kernel(
+    dims,
+    ens_ref,
+    gain_ref,
+    w_proj_any,
+    w_out_any,
+    conv_any,
+    cot_ref,
+    result_ref,
+    grad_ref,
+    w_proj_ref,
+    w_out_ref,
+    conv_ref,
+    out_buf,
+    in_buf,
+    halo_cot,
+    halo_up,
+    edge_cot,
+    edge_up,
+    field_ref,
+    gf_ref,
+    load_sem,
+    ex_send,
+    ex_recv,
+    halo_send,
+    halo_recv,
+):
+    mem, lat, lon, channels, peers, lats, lons = dims
+    cells = mem * lat * lon
+    members = mem * peers
+    me = lax.axis_index("member")
+    my_lat = lax.axis_index("lat")
+    my_lon = lax.axis_index("lon")
+
+    loads = [
+        pltpu.make_async_copy(src, dst, load_sem.at[i])
+        for i, (src, dst) in enumerate(
+            ((conv_any, conv_ref), (w_proj_any, w_proj_ref), (w_out_any, w_out_ref))
+        )
+    ]
+    for load in loads:
+        load.start()
+
+    def partner(j):
+        return {"member": lax.rem(me + j, peers)}
+
+    def near(d_lat, d_lon):
+        return {
+            "lat": lax.rem(my_lat + d_lat + lats, lats),
+            "lon": lax.rem(my_lon + d_lon + lons, lons),
+        }
+
+    around = [(a, b) for a in (-1, 0, 1) for b in (-1, 0, 1) if (a, b) != (0, 0)]
+    barrier = pltpu.get_barrier_semaphore()
+    for j in range(1, peers):
+        pl.semaphore_signal(barrier, inc=1, device_id=partner(j), device_id_type=MESH)
+    for d_lat, d_lon in around:
+        pl.semaphore_signal(barrier, inc=1, device_id=near(d_lat, d_lon), device_id_type=MESH)
+
+    def home_source(i):
+        j, m, a = i // (mem * lat), (i // lat) % mem, i % lat
+        return (m * lat + a) * lon + lax.rem(me + j, peers)
+
+    def home_target(i):
+        m, a, b = i // (lat * lon), (i // lon) % lat, i % lon
+        return lax.rem(b - me + peers, peers) * (mem * lat) + m * lat + a
+
+    def cell_source(i):
+        c, j, m = i // members, (i // mem) % peers, i % mem
+        return (j * mem + m) * lat + c
+
+    def cell_target(i):
+        j, m, c = i // (mem * lat), (i // lat) % mem, i % lat
+        return (c * peers + j) * mem + m
+
+    def edge_source(i):
+        count = mem * lat
+        return (i % count) * lon + (i // count) * (lon - 1)
+
+    square = (cells, cells)
+    home_out = one_hot(square, home_source)
+    home_in = one_hot(square, home_target)
+    cell_in = one_hot(square, cell_source)
+    cell_out = one_hot(square, cell_target)
+    edges = one_hot((2 * mem * lat, cells), edge_source)
+
+    def exchange(kind, sign):
+        return [
+            pltpu.make_async_remote_copy(
+                src_ref=out_buf.at[kind, j],
+                dst_ref=in_buf.at[kind, j],
+                send_sem=ex_send.at[kind],
+                recv_sem=ex_recv.at[kind],
+                device_id=partner(j if sign > 0 else peers - j),
+                device_id_type=MESH,
+            )
+            for j in range(1, peers)
+        ]
+
+    def exchange_all(kind):
+        return pltpu.make_async_remote_copy(
+            src_ref=out_buf.at[kind, pl.ds(1, peers - 1)],
+            dst_ref=in_buf.at[kind, pl.ds(1, peers - 1)],
+            send_sem=ex_send.at[kind],
+            recv_sem=ex_recv.at[kind],
+            device_id=partner(1),
+            device_id_type=MESH,
+        )
+
+    def send(kind, order, rows, sign):
+        packed = pack(nn(order, rows), peers)
+        out_buf[kind] = packed
+        in_buf[kind, 0] = packed[0]
+        for copy in exchange(kind, sign):
+            copy.start()
+
+    def receive(kind, order):
+        exchange_all(kind).wait_recv()
+        return nn(order, unpack(in_buf[kind]))
+
+    def halo_copies(slot, rows_ref, edge_ref, halo):
+        copies = []
+        for side, (d_lat, a) in enumerate(((1, lat - 1), (-1, 0))):
+            copies.append(
+                pltpu.make_async_remote_copy(
+                    src_ref=rows_ref.at[:, a],
+                    dst_ref=halo.at[:, 0 if side == 0 else lat + 1],
+                    send_sem=halo_send.at[slot, side],
+                    recv_sem=halo_recv.at[slot, side],
+                    device_id=near(d_lat, 0),
+                    device_id_type=MESH,
+                )
+            )
+        for d_lat in (-1, 0, 1):
+            for d_lon in (-1, 1):
+                copies.append(
+                    pltpu.make_async_remote_copy(
+                        src_ref=edge_ref,
+                        dst_ref=halo.at[0 if d_lon > 0 else 1, lat + 2 + 1 - d_lat],
+                        send_sem=halo_send.at[slot, 2],
+                        recv_sem=halo_recv.at[slot, 2],
+                        device_id=near(d_lat, d_lon),
+                        device_id_type=MESH,
+                    )
+                )
+        return copies
+
+    def halo_cols(slot, halo):
+        cols = halo.at[:, pl.ds(lat + 2, 3)]
+        return pltpu.make_async_remote_copy(
+            src_ref=cols,
+            dst_ref=cols,
+            send_sem=halo_send.at[slot, 2],
+            recv_sem=halo_recv.at[slot, 2],
+            device_id=near(0, 1),
+            device_id_type=MESH,
+        )
+
+    def wait_halo(slot, copies, halo):
+        copies[0].wait_recv()
+        copies[1].wait_recv()
+        halo_cols(slot, halo).wait_recv()
+
+    def wait_halo_sent(slot, copies, halo):
+        copies[0].wait_send()
+        copies[1].wait_send()
+        halo_cols(slot, halo).wait_send()
+
+    strip = lat + 2
+    extra = 3 * lon
+
+    def column_source(shift):
+        def source(i):
+            a, b = i // lon, i % lon
+            inner = a * lon + b + shift
+            which = jnp.where(a == 0, 0, jnp.where(a == strip - 1, 2, 1))
+            row = jnp.where(a == 0, lat - 1, jnp.where(a == strip - 1, 0, a - 1))
+            base = (mem * lat if shift < 0 else 0) + row
+            outer = strip * lon + which * lon + base
+            edge = b == (0 if shift < 0 else lon - 1)
+            return jnp.where(edge, outer, inner), edge
+
+        return source
+
+    def shifted(halo, body, m, shift):
+        low = jnp.where(my_lat > 0, halo[m, 0].astype(F32), 0.0).astype(BF)
+        high = jnp.where(my_lat < lats - 1, halo[m, strip - 1].astype(F32), 0.0).astype(BF)
+        middle = body(m)
+        field = jnp.concatenate([low, middle, high], axis=0)
+        if shift == 0:
+            return field
+        side = 0 if shift < 0 else 1
+        columns = halo[side, lat + 2 : lat + 5].reshape(extra, channels)
+        shape = (strip * lon, strip * lon + extra)
+        source, edge = column_source(shift)(iota(shape, 0))
+        source = jnp.where(edge, source + m * lat, source)
+        row = iota(shape, 0) // lon
+        open_row = jnp.logical_and(
+            jnp.logical_or(row > 0, my_lat > 0),
+            jnp.logical_or(row < strip - 1, my_lat < lats - 1),
+        )
+        pick = jnp.where(jnp.logical_and(iota(shape, 1) == source, open_row), 1.0, 0.0).astype(BF)
+        return nn(pick, jnp.concatenate([field, columns], axis=0)).astype(BF)
+
+    def conv(halo, body, adjoint):
+        total = None
         for c in range(3):
-            i, j = (2 - r, 2 - c) if adjoint else (r, c)
-            window = wide[:, i : i + lat, j : j + lon].reshape(mem * lat * lon, channels)
-            term = nt(window, kernel[r, c]) if adjoint else nn(window, kernel[r, c])
-            total = term if total is None else total + term
-    return total
-
-
-def to_cells(rows):
-    mem, lat, lon, channels = rows.shape
-    count = lax.axis_size("member")
-    out = rows.reshape(mem, lat, count, lon // count, channels).transpose(2, 1, 3, 0, 4)
-    out = lax.all_to_all(out, "member", 0, 0, tiled=True)
-    return out.transpose(1, 2, 0, 3, 4).reshape(-1, channels)
-
-
-def to_home(rows, shape):
-    mem, lat, lon, channels = shape
-    count = lax.axis_size("member")
-    out = rows.reshape(lat, lon // count, count, mem, channels).transpose(2, 0, 1, 3, 4)
-    out = lax.all_to_all(out, "member", 0, 0, tiled=True)
-    return out.transpose(3, 1, 0, 2, 4).reshape(shape)
+            shift = 1 - c if adjoint else c - 1
+            wide = [shifted(halo, body, m, shift) for m in range(mem)]
+            for r in range(3):
+                start = (2 - r if adjoint else r) * lon
+                window = jnp.concatenate([w[start : start + lat * lon] for w in wide], axis=0)
+                term = nt(window, conv_ref[r, c]) if adjoint else nn(window, conv_ref[r, c])
+                total = term if total is None else total + term
+        return total
+
+    def cot_body(m):
+        return cot_ref[m].reshape(lat * lon, channels)
+
+    def up_body(m):
+        return field_ref[m].reshape(lat * lon, channels)
+
+    ens = ens_ref[...].reshape(cells, channels)
+    cot = cot_ref[...].reshape(cells, channels)
+    packed = pack(nn(home_out, ens), peers)
+    out_buf[X] = packed
+    in_buf[X, 0] = packed[0]
+    edge_cot[...] = nn(edges, cot).astype(BF)
+    pl.semaphore_wait(barrier, peers - 1 + len(around))
+    for copy in exchange(X, 1):
+        copy.start()
+    cot_copies = halo_copies(0, cot_ref, edge_cot, halo_cot)
+    for copy in cot_copies:
+        copy.start()
+
+    ones = head_blocks(channels, members).astype(BF)
+    gain = gain_ref[...]
+    loads[0].wait()
+    wait_halo(0, cot_copies, halo_cot)
+    grad_field = cot.astype(F32) + conv(halo_cot, cot_body, True)
+    gf_ref[...] = grad_field
+    send(G, home_out, grad_field.astype(BF), 1)
+
+    loads[1].wait()
+    loads[2].wait()
+    w_proj = w_proj_ref[...]
+    w_out = w_out_ref[...]
+    x = receive(X, cell_in).astype(BF)
+    updated, saved = cell_forward(x, gain, w_proj, w_out, ones, members)
+    send(U, cell_out, updated, -1)
+
+    grads = receive(G, cell_in).astype(BF)
+    grad_inputs = cell_backward(grads, saved, gain, w_proj, w_out, ones, members)
+    send(B, cell_out, grad_inputs.astype(BF), -1)
+
+    field = receive(U, home_in)
+    field_ref[...] = field.astype(BF).reshape(field_ref.shape)
+    edge_up[...] = nn(edges, field.astype(BF)).astype(BF)
+    up_copies = halo_copies(1, field_ref, edge_up, halo_up)
+    for copy in up_copies:
+        copy.start()
+    wait_halo(1, up_copies, halo_up)
+    result = field + conv(halo_up, up_body, False)
+    result_ref[...] = result.astype(BF).reshape(result_ref.shape)
+
+    back = receive(B, home_in)
+    grad_ref[...] = (gf_ref[...] + back).astype(BF).reshape(grad_ref.shape)
+
+    for kind in (X, G, U, B):
+        exchange_all(kind).wait_send()
+    wait_halo_sent(0, cot_copies, halo_cot)
+    wait_halo_sent(1, up_copies, halo_up)
+
+
+MESH = pl.DeviceIdType.MESH
 
 
 def per_device(ensemble, norm_gain, project_weight, output_weight, conv_kernel, cotangent):
     mem, lat, lon, channels = ensemble.shape
-    members = mem * lax.axis_size("member")
-    ones = head_blocks(channels, members).astype(BF)
-    gain = norm_gain.reshape(1, channels)
-    x = to_cells(ensemble)
-    updated, saved = cell_forward(x, gain, project_weight, output_weight, ones, members)
-    field = to_home(updated, ensemble.shape)
-    grad_field = cotangent.astype(F32).reshape(-1, channels) + conv_taps(cotangent, conv_kernel, True)
-    grad_cells = to_cells(grad_field.astype(BF).reshape(ensemble.shape))
-    grad_inputs = cell_backward(grad_cells, saved, gain, project_weight, output_weight, ones, members)
-    result = field.astype(F32).reshape(-1, channels) + conv_taps(field, conv_kernel, False)
-    back = to_home(grad_inputs.astype(BF), ensemble.shape).astype(F32).reshape(-1, channels)
-    return (
-        result.astype(BF).reshape(ensemble.shape),
-        (grad_field + back).astype(BF).reshape(ensemble.shape),
+    peers = lax.axis_size("member")
+    dims = (mem, lat, lon, channels, peers, lax.axis_size("lat"), lax.axis_size("lon"))
+    vmem = pl.BlockSpec(memory_space=pltpu.VMEM)
+    anywhere = pl.BlockSpec(memory_space=pl.ANY)
+    chunk = (4, peers, 2 * mem * lat, channels // 2)
+    halo = (mem, lat + 5, lon, channels)
+    field = jax.ShapeDtypeStruct(ensemble.shape, BF)
+    return pl.pallas_call(
+        functools.partial(kernel, dims),
+        out_shape=(field, field),
+        in_specs=[vmem, vmem, anywhere, anywhere, anywhere, vmem],
+        out_specs=(vmem, vmem),
+        scratch_shapes=[
+            pltpu.VMEM(project_weight.shape, BF),
+            pltpu.VMEM(output_weight.shape, BF),
+            pltpu.VMEM(conv_kernel.shape, BF),
+            pltpu.VMEM(chunk, BF),
+            pltpu.VMEM(chunk, BF),
+            pltpu.VMEM(halo, BF),
+            pltpu.VMEM(halo, BF),
+            pltpu.VMEM((2 * mem * lat, channels), BF),
+            pltpu.VMEM((2 * mem * lat, channels), BF),
+            pltpu.VMEM(ensemble.shape, BF),
+            pltpu.VMEM((mem * lat * lon, channels), F32),
+            pltpu.SemaphoreType.DMA((3,)),
+            pltpu.SemaphoreType.DMA((4,)),
+            pltpu.SemaphoreType.DMA((4,)),
+            pltpu.SemaphoreType.DMA((2, 3)),
+            pltpu.SemaphoreType.DMA((2, 3)),
+        ],
+        compiler_params=pltpu.CompilerParams(collective_id=0, has_side_effects=True),
+    )(
+        ensemble,
+        norm_gain.reshape(1, channels),
+        project_weight,
+        output_weight,
+        conv_kernel,
+        cotangent,
     )
 
 

time: 91.1 us -> 36.1 us (0.40)
  starting transfers between devices: 52.6 us -> 0 us
  Pallas kernels: 0 us -> 32.3 us
  matrix products: 17 us -> 0 us
  waiting for transfers between devices: 8.78 us -> 0 us
  other arithmetic: 4.03 us -> 0 us
  local copies, waits for them, and re-layouts: 6.26 us -> 2.95 us
  between operations: 1.66 us -> 0.64 us
    all_to_all x4 -> x0, starting transfers between devices: 34.5 us -> none  [the longest x2 19.1 us: to_cells(): out = lax.all_to_all(out, 'member', 0, 0, tiled=True)]
    pallas_call x0 -> x1, Pallas kernels: none -> 32.3 us  [per_device(): pl.pallas_call(functools.partial(kernel, dims), out_shape=(field, field),...]
    ppermute x8 -> x0, starting transfers between devices: 18.1 us -> none  [the longest x4 14.9 us: padded(): lax.ppermute(lax.slice_in_dim(block, block.shape[dim] - 1, None, axis=dim...]
    dot_general x52 -> x0, matrix products: 17 us -> none  [mm(): return lax.dot_general(a, b, (dims, ((), ())), preferred_element_type=F32)]
    ppermute x8 -> x0, waiting for transfers between devices: 6.04 us -> none  [the longest x4 5.4 us: padded(): high = lax.ppermute(lax.slice_in_dim(block, 0, 1, axis=dim), axis, backward)]
    all_to_all x4 -> x0, waiting for transfers between devices: 2.74 us -> none  [the longest x2 2.49 us: to_cells(): out = lax.all_to_all(out, 'member', 0, 0, tiled=True)]
    concatenate x4 -> x0, other arithmetic: 2.11 us -> none  [padded(): block = jnp.concatenate([low, block, high], axis=dim)]
    reshape x5 -> x0, local copies, waits for them, and re-layouts: 1.46 us -> none  [the longest x4 1.43 us: to_home(): rows.reshape(lat, lon // count, count, mem, channels)]
  transfers between devices with their start and end apart: 12 -> 0, of which waited for: 5 -> 0; matrix products, arithmetic and copies ran while one was open for 26% -> 0% of each run, Pallas kernels for 0% -> 0%
where the time goes in v2:
time: 36.1 us; the launch traced here: 35.8 us
  Pallas kernels  32.3 us (89%)
  local copies, waits for them, and re-layouts  2.95 us (8%)
  between operations  0.64 us (2%)
    pallas_call x1, Pallas kernels, per_device(): pl.pallas_call(functools.partial(kernel, dims), out_shape=(field, field),...  32.3 us
    unnamed x2, local copies, waits for them, and re-layouts  2.95 us

profile of v2, /device:TPU:1, one launch (start us, length us, event | category | flops | bytes accessed | tf_op | source)
XLA Modules:
  0.0 35.8 jit_solution(16375911653404659138)
XLA Ops:
  0.6 32.3 %shard_map.77 = (bf16[2,4,16,256]{3,2,1,0:T(8,128)(2,1)}, bf16[2,4,16,256]{3,2,1,0:T(8,128)(2,1)}) custom-call(bf16[2,4,16,256]{3,2,1,0:T(8,128)(2,1)} %ens_ref.1, f32[1,256]{1,0:T(1,128)} %bitcast.1, bf16[256,768]{1,0:T(8,128)(2,1)} %w_proj_any.1, bf16[256,256]{1,0:T(8,128)(2,1)} %w_out_any.1, bf16[3,3,256,256]{3,2,1,0:T(8,128)(2,1)} %conv_any.1, ...), custom_call_target="tpu_custom_call" | custom-call | tf_op jit(solution)/shard_map/pallas_call | solution.py:434
  32.9 1.5 %copy.10 = bf16[2,4,16,256]{3,2,1,0:T(8,128)(2,1)} copy(bf16[2,4,16,256]{3,2,1,0:T(8,128)(2,1)} %get-tuple-element.4) | data formatting | bytes 131072
  34.4 1.5 %copy.11 = bf16[2,4,16,256]{3,2,1,0:T(8,128)(2,1)} copy(bf16[2,4,16,256]{3,2,1,0:T(8,128)(2,1)} %get-tuple-element.5) | data formatting | bytes 131072

commit v3 on v2

--- a/solution.py
+++ b/solution.py
@@ -147,14 +147,17 @@
 
 def kernel(
     dims,
-    ens_ref,
-    gain_ref,
+    ens_any,
+    gain_any,
     w_proj_any,
     w_out_any,
     conv_any,
-    cot_ref,
+    cot_any,
     result_ref,
     grad_ref,
+    ens_ref,
+    cot_ref,
+    gain_ref,
     w_proj_ref,
     w_out_ref,
     conv_ref,
@@ -179,11 +182,16 @@
     my_lat = lax.axis_index("lat")
     my_lon = lax.axis_index("lon")
 
+    pairs = (
+        (ens_any, ens_ref),
+        (cot_any, cot_ref),
+        (conv_any, conv_ref),
+        (w_proj_any, w_proj_ref),
+        (w_out_any, w_out_ref),
+        (gain_any, gain_ref),
+    )
     loads = [
-        pltpu.make_async_copy(src, dst, load_sem.at[i])
-        for i, (src, dst) in enumerate(
-            ((conv_any, conv_ref), (w_proj_any, w_proj_ref), (w_out_any, w_out_ref))
-        )
+        pltpu.make_async_copy(src, dst, load_sem.at[i]) for i, (src, dst) in enumerate(pairs)
     ]
     for load in loads:
         load.start()
@@ -199,7 +207,8 @@
 
     around = [(a, b) for a in (-1, 0, 1) for b in (-1, 0, 1) if (a, b) != (0, 0)]
     barrier = pltpu.get_barrier_semaphore()
-    for j in range(1, peers):
+    far_first = sorted(range(1, peers), key=lambda j: -min(j, peers - j))
+    for j in far_first:
         pl.semaphore_signal(barrier, inc=1, device_id=partner(j), device_id_type=MESH)
     for d_lat, d_lon in around:
         pl.semaphore_signal(barrier, inc=1, device_id=near(d_lat, d_lon), device_id_type=MESH)
@@ -241,7 +250,7 @@
                 device_id=partner(j if sign > 0 else peers - j),
                 device_id_type=MESH,
             )
-            for j in range(1, peers)
+            for j in far_first
         ]
 
     def exchange_all(kind):
@@ -367,7 +376,9 @@
     def up_body(m):
         return field_ref[m].reshape(lat * lon, channels)
 
+    loads[0].wait()
     ens = ens_ref[...].reshape(cells, channels)
+    loads[1].wait()
     cot = cot_ref[...].reshape(cells, channels)
     packed = pack(nn(home_out, ens), peers)
     out_buf[X] = packed
@@ -381,15 +392,15 @@
         copy.start()
 
     ones = head_blocks(channels, members).astype(BF)
-    gain = gain_ref[...]
-    loads[0].wait()
+    loads[2].wait()
     wait_halo(0, cot_copies, halo_cot)
     grad_field = cot.astype(F32) + conv(halo_cot, cot_body, True)
     gf_ref[...] = grad_field
     send(G, home_out, grad_field.astype(BF), 1)
 
-    loads[1].wait()
-    loads[2].wait()
+    for load in loads[3:]:
+        load.wait()
+    gain = gain_ref[...]
     w_proj = w_proj_ref[...]
     w_out = w_out_ref[...]
     x = receive(X, cell_in).astype(BF)
@@ -419,7 +430,19 @@
     wait_halo_sent(1, up_copies, halo_up)
 
 
+def store_kernel(result_in, grad_in, result_out, grad_out, sem):
+    copies = [
+        pltpu.make_async_copy(result_in, result_out, sem.at[0]),
+        pltpu.make_async_copy(grad_in, grad_out, sem.at[1]),
+    ]
+    for copy in copies:
+        copy.start()
+    for copy in copies:
+        copy.wait()
+
+
 MESH = pl.DeviceIdType.MESH
+LIMIT = 16 * 1024 * 1024
 
 
 def per_device(ensemble, norm_gain, project_weight, output_weight, conv_kernel, cotangent):
@@ -431,12 +454,15 @@
     chunk = (4, peers, 2 * mem * lat, channels // 2)
     halo = (mem, lat + 5, lon, channels)
     field = jax.ShapeDtypeStruct(ensemble.shape, BF)
-    return pl.pallas_call(
+    outs = pl.pallas_call(
         functools.partial(kernel, dims),
         out_shape=(field, field),
-        in_specs=[vmem, vmem, anywhere, anywhere, anywhere, vmem],
+        in_specs=[pl.BlockSpec(memory_space=pltpu.HBM)] * 6,
         out_specs=(vmem, vmem),
         scratch_shapes=[
+            pltpu.VMEM(ensemble.shape, BF),
+            pltpu.VMEM(ensemble.shape, BF),
+            pltpu.VMEM((1, channels), F32),
             pltpu.VMEM(project_weight.shape, BF),
             pltpu.VMEM(output_weight.shape, BF),
             pltpu.VMEM(conv_kernel.shape, BF),
@@ -448,21 +474,36 @@
             pltpu.VMEM((2 * mem * lat, channels), BF),
             pltpu.VMEM(ensemble.shape, BF),
             pltpu.VMEM((mem * lat * lon, channels), F32),
-            pltpu.SemaphoreType.DMA((3,)),
+            pltpu.SemaphoreType.DMA((6,)),
             pltpu.SemaphoreType.DMA((4,)),
             pltpu.SemaphoreType.DMA((4,)),
             pltpu.SemaphoreType.DMA((2, 3)),
             pltpu.SemaphoreType.DMA((2, 3)),
         ],
-        compiler_params=pltpu.CompilerParams(collective_id=0, has_side_effects=True),
+        compiler_params=pltpu.CompilerParams(
+            collective_id=0, has_side_effects=True, vmem_limit_bytes=LIMIT
+        ),
     )(
-        ensemble,
-        norm_gain.reshape(1, channels),
-        project_weight,
-        output_weight,
-        conv_kernel,
-        cotangent,
+        *(
+            pltpu.with_memory_space_constraint(value, pltpu.HBM)
+            for value in (
+                ensemble,
+                norm_gain.reshape(1, channels),
+                project_weight,
+                output_weight,
+                conv_kernel,
+                cotangent,
+            )
+        )
     )
+    return pl.pallas_call(
+        store_kernel,
+        out_shape=(field, field),
+        in_specs=[vmem, vmem],
+        out_specs=(anywhere, anywhere),
+        scratch_shapes=[pltpu.SemaphoreType.DMA((2,))],
+        compiler_params=pltpu.CompilerParams(vmem_limit_bytes=LIMIT),
+    )(*outs)
 
 
 def solution(mesh):

time: 36.1 us -> 31.5 us (0.87)
  local copies, waits for them, and re-layouts: 2.95 us -> 0 us
  Pallas kernels: 32.3 us -> 30.7 us
    unnamed x2 -> x0, local copies, waits for them, and re-layouts: 2.95 us -> none
    pallas_call x1, Pallas kernels: 32.3 us -> 30.1 us  [per_device(): pl.pallas_call(functools.partial(kernel, dims), out_shape=(field, field),...]
    pallas_call x0 -> x1, Pallas kernels: none -> 0.67 us  [per_device(): pl.pallas_call(store_kernel, out_shape=(field, field), in_specs=[vmem, vm...]
where the time goes in v3:
time: 31.5 us; the launch traced here: 31.4 us
  Pallas kernels  30.7 us (97%)
  between operations  0.64 us (2%)
    pallas_call x1, Pallas kernels, per_device(): pl.pallas_call(functools.partial(kernel, dims), out_shape=(field, field),...  30.1 us
    pallas_call x1, Pallas kernels, per_device(): pl.pallas_call(store_kernel, out_shape=(field, field), in_specs=[vmem, vm...  0.67 us

profile of v3, /device:TPU:1, one launch (start us, length us, event | category | flops | bytes accessed | tf_op | source)
XLA Modules:
  0.0 31.4 jit_solution(292417752265559645)
XLA Ops:
  0.6 30.1 %shard_map.77 = (bf16[2,4,16,256]{3,2,1,0:T(8,128)(2,1)S(1)}, bf16[2,4,16,256]{3,2,1,0:T(8,128)(2,1)S(1)}) custom-call(bf16[2,4,16,256]{3,2,1,0:T(8,128)(2,1)} %ens_any.1, f32[1,256]{1,0:T(1,128)} %bitcast.1, bf16[256,768]{1,0:T(8,128)(2,1)} %w_proj_any.1, bf16[256,256]{1,0:T(8,128)(2,1)} %w_out_any.1, bf16[3,3,256,256]{3,2,1,0:T(8,128)(2,1)} %conv_any.1, ...), custom_call_target="tpu_custom_call" | custom-call | tf_op jit(solution)/shard_map/pallas_call | solution.py:457
  30.7 0.7 %shard_map.78 = (bf16[2,4,16,256]{3,2,1,0:T(8,128)(2,1)}, bf16[2,4,16,256]{3,2,1,0:T(8,128)(2,1)}) custom-call(bf16[2,4,16,256]{3,2,1,0:T(8,128)(2,1)S(1)} %get-tuple-element.4.result_in, bf16[2,4,16,256]{3,2,1,0:T(8,128)(2,1)S(1)} %get-tuple-element.5.grad_in), custom_call_target="tpu_custom_call" | custom-call | tf_op jit(solution)/shard_map/pallas_call | solution.py:499

commit v4 on v3

--- a/solution.py
+++ b/solution.py
@@ -174,6 +174,7 @@
     ex_recv,
     halo_send,
     halo_recv,
+    flag,
 ):
     mem, lat, lon, channels, peers, lats, lons = dims
     cells = mem * lat * lon
@@ -208,8 +209,16 @@
     around = [(a, b) for a in (-1, 0, 1) for b in (-1, 0, 1) if (a, b) != (0, 0)]
     barrier = pltpu.get_barrier_semaphore()
     far_first = sorted(range(1, peers), key=lambda j: -min(j, peers - j))
-    for j in far_first:
-        pl.semaphore_signal(barrier, inc=1, device_id=partner(j), device_id_type=MESH)
+    ring = peers // 2
+    my_z, my_y = me // 2, lax.rem(me, 2)
+
+    def along(dz):
+        return {"member": lax.rem(my_z + dz + ring, ring) * 2 + my_y}
+
+    twin = {"member": my_z * 2 + 1 - my_y}
+    close = [along(dz) for dz in (-2, 2, -1, 1)] + [twin]
+    for device in close:
+        pl.semaphore_signal(barrier, inc=1, device_id=device, device_id_type=MESH)
     for d_lat, d_lon in around:
         pl.semaphore_signal(barrier, inc=1, device_id=near(d_lat, d_lon), device_id_type=MESH)
 
@@ -384,11 +393,17 @@
     out_buf[X] = packed
     in_buf[X, 0] = packed[0]
     edge_cot[...] = nn(edges, cot).astype(BF)
-    pl.semaphore_wait(barrier, peers - 1 + len(around))
-    for copy in exchange(X, 1):
-        copy.start()
+    pl.semaphore_wait(barrier, len(close) + len(around))
+    for device in (along(-2), along(2), twin):
+        pl.semaphore_signal(flag.at[0], inc=1, device_id=device, device_id_type=MESH)
     cot_copies = halo_copies(0, cot_ref, edge_cot, halo_cot)
     for copy in cot_copies:
+        copy.start()
+    pl.semaphore_wait(flag.at[0], 3)
+    for device in (along(-2), along(2)):
+        pl.semaphore_signal(flag.at[1], inc=1, device_id=device, device_id_type=MESH)
+    pl.semaphore_wait(flag.at[1], 2)
+    for copy in exchange(X, 1):
         copy.start()
 
     ones = head_blocks(channels, members).astype(BF)
@@ -479,6 +494,7 @@
             pltpu.SemaphoreType.DMA((4,)),
             pltpu.SemaphoreType.DMA((2, 3)),
             pltpu.SemaphoreType.DMA((2, 3)),
+            pltpu.SemaphoreType.REGULAR((2,)),
         ],
         compiler_params=pltpu.CompilerParams(
             collective_id=0, has_side_effects=True, vmem_limit_bytes=LIMIT

time: 31.5 us -> 32.9 us (1.044)
  Pallas kernels: 30.7 us -> 32.2 us
    pallas_call x1, Pallas kernels: 30.1 us -> 31.5 us  [per_device(): pl.pallas_call(functools.partial(kernel, dims), out_shape=(field, field),...]
where the time goes in v4:
time: 32.9 us; the launch traced here: 32.8 us
  Pallas kernels  32.2 us (98%)
  between operations  0.64 us (2%)
    pallas_call x1, Pallas kernels, per_device(): pl.pallas_call(functools.partial(kernel, dims), out_shape=(field, field),...  31.5 us
    pallas_call x1, Pallas kernels, per_device(): pl.pallas_call(store_kernel, out_shape=(field, field), in_specs=[vmem, vm...  0.67 us

profile of v4, /device:TPU:1, one launch (start us, length us, event | category | flops | bytes accessed | tf_op | source)
XLA Modules:
  0.0 32.8 jit_solution(3810773636866609405)
XLA Ops:
  0.6 31.5 %shard_map.77 = (bf16[2,4,16,256]{3,2,1,0:T(8,128)(2,1)S(1)}, bf16[2,4,16,256]{3,2,1,0:T(8,128)(2,1)S(1)}) custom-call(bf16[2,4,16,256]{3,2,1,0:T(8,128)(2,1)} %ens_any.1, f32[1,256]{1,0:T(1,128)} %bitcast.1, bf16[256,768]{1,0:T(8,128)(2,1)} %w_proj_any.1, bf16[256,256]{1,0:T(8,128)(2,1)} %w_out_any.1, bf16[3,3,256,256]{3,2,1,0:T(8,128)(2,1)} %conv_any.1, ...), custom_call_target="tpu_custom_call" | custom-call | tf_op jit(solution)/shard_map/pallas_call | solution.py:472
  32.1 0.7 %shard_map.78 = (bf16[2,4,16,256]{3,2,1,0:T(8,128)(2,1)}, bf16[2,4,16,256]{3,2,1,0:T(8,128)(2,1)}) custom-call(bf16[2,4,16,256]{3,2,1,0:T(8,128)(2,1)S(1)} %get-tuple-element.4.result_in, bf16[2,4,16,256]{3,2,1,0:T(8,128)(2,1)S(1)} %get-tuple-element.5.grad_in), custom_call_target="tpu_custom_call" | custom-call | tf_op jit(solution)/shard_map/pallas_call | solution.py:515

commit v5 on v4

--- a/solution.py
+++ b/solution.py
@@ -164,16 +164,24 @@
     out_buf,
     in_buf,
     halo_cot,
-    halo_up,
     edge_cot,
-    edge_up,
-    field_ref,
     gf_ref,
+    rim_out,
+    rim_in,
+    side_in,
+    corner_in,
+    column_ref,
     load_sem,
     ex_send,
     ex_recv,
     halo_send,
     halo_recv,
+    rim_send,
+    rim_recv,
+    side_send,
+    side_recv,
+    corner_send,
+    corner_recv,
     flag,
 ):
     mem, lat, lon, channels, peers, lats, lons = dims
@@ -213,10 +221,11 @@
     my_z, my_y = me // 2, lax.rem(me, 2)
 
     def along(dz):
-        return {"member": lax.rem(my_z + dz + ring, ring) * 2 + my_y}
+        return {"member": lax.rem(my_z + dz, ring) * 2 + my_y}
 
     twin = {"member": my_z * 2 + 1 - my_y}
-    close = [along(dz) for dz in (-2, 2, -1, 1)] + [twin]
+    z_steps = sorted(range(1, ring), key=lambda j: -min(j, ring - j))
+    close = [along(dz) for dz in z_steps] + [twin]
     for device in close:
         pl.semaphore_signal(barrier, inc=1, device_id=device, device_id_type=MESH)
     for d_lat, d_lon in around:
@@ -283,95 +292,288 @@
         exchange_all(kind).wait_recv()
         return nn(order, unpack(in_buf[kind]))
 
-    def halo_copies(slot, rows_ref, edge_ref, halo):
-        copies = []
-        for side, (d_lat, a) in enumerate(((1, lat - 1), (-1, 0))):
+    has_low, has_high = my_lat > 0, my_lat < lats - 1
+
+    def halo_group(d_lat):
+        which = 1 - d_lat
+        copies = [
+            pltpu.make_async_remote_copy(
+                src_ref=edge_cot,
+                dst_ref=halo_cot.at[0 if d_lon > 0 else 1, lat + 2 + which],
+                send_sem=halo_send.at[which],
+                recv_sem=halo_recv.at[which],
+                device_id=near(d_lat, d_lon),
+                device_id_type=MESH,
+            )
+            for d_lon in (-1, 1)
+        ]
+        if d_lat:
             copies.append(
                 pltpu.make_async_remote_copy(
-                    src_ref=rows_ref.at[:, a],
-                    dst_ref=halo.at[:, 0 if side == 0 else lat + 1],
-                    send_sem=halo_send.at[slot, side],
-                    recv_sem=halo_recv.at[slot, side],
+                    src_ref=cot_ref.at[:, lat - 1 if d_lat > 0 else 0],
+                    dst_ref=halo_cot.at[:, 0 if d_lat > 0 else lat + 1],
+                    send_sem=halo_send.at[3 + (which > 1)],
+                    recv_sem=halo_recv.at[3 + (which > 1)],
                     device_id=near(d_lat, 0),
                     device_id_type=MESH,
                 )
             )
-        for d_lat in (-1, 0, 1):
-            for d_lon in (-1, 1):
-                copies.append(
-                    pltpu.make_async_remote_copy(
-                        src_ref=edge_ref,
-                        dst_ref=halo.at[0 if d_lon > 0 else 1, lat + 2 + 1 - d_lat],
-                        send_sem=halo_send.at[slot, 2],
-                        recv_sem=halo_recv.at[slot, 2],
-                        device_id=near(d_lat, d_lon),
-                        device_id_type=MESH,
-                    )
-                )
         return copies
 
-    def halo_cols(slot, halo):
-        cols = halo.at[:, pl.ds(lat + 2, 3)]
+    def halo_columns(which):
+        columns = halo_cot.at[:, lat + 2 + which]
         return pltpu.make_async_remote_copy(
-            src_ref=cols,
-            dst_ref=cols,
-            send_sem=halo_send.at[slot, 2],
-            recv_sem=halo_recv.at[slot, 2],
+            src_ref=columns,
+            dst_ref=columns,
+            send_sem=halo_send.at[which],
+            recv_sem=halo_recv.at[which],
             device_id=near(0, 1),
             device_id_type=MESH,
         )
 
-    def wait_halo(slot, copies, halo):
-        copies[0].wait_recv()
-        copies[1].wait_recv()
-        halo_cols(slot, halo).wait_recv()
-
-    def wait_halo_sent(slot, copies, halo):
-        copies[0].wait_send()
-        copies[1].wait_send()
-        halo_cols(slot, halo).wait_send()
+    def start_halo():
+        @pl.when(has_high)
+        def _():
+            for copy in halo_group(1):
+                copy.start()
+
+        @pl.when(has_low)
+        def _():
+            for copy in halo_group(-1):
+                copy.start()
+
+        for copy in halo_group(0):
+            copy.start()
+
+    def wait_halo():
+        halo_columns(1).wait_recv()
+
+        @pl.when(has_low)
+        def _():
+            halo_columns(0).wait_recv()
+            halo_group(1)[2].wait_recv()
+
+        @pl.when(has_high)
+        def _():
+            halo_columns(2).wait_recv()
+            halo_group(-1)[2].wait_recv()
+
+    def wait_halo_sent():
+        halo_columns(1).wait_send()
+
+        @pl.when(has_high)
+        def _():
+            halo_columns(0).wait_send()
+            halo_group(1)[2].wait_send()
+
+        @pl.when(has_low)
+        def _():
+            halo_columns(2).wait_send()
+            halo_group(-1)[2].wait_send()
+
+    every = [0] + far_first
+
+    def shift_of(rim):
+        return 1 if rim == 0 else lats - 1
+
+    def home_of(j, d_lat, d_lon):
+        return {
+            "member": lax.rem(me + peers - j, peers),
+            "lat": lax.rem(my_lat + d_lat, lats),
+            "lon": lax.rem(my_lon + d_lon, lons),
+        }
+
+    def rim_copies(rim):
+        return [
+            pltpu.make_async_remote_copy(
+                src_ref=rim_out.at[rim, j],
+                dst_ref=rim_in.at[rim, j],
+                send_sem=rim_send.at[rim],
+                recv_sem=rim_recv.at[rim],
+                device_id=home_of(j, shift_of(rim), 0),
+                device_id_type=MESH,
+            )
+            for j in every
+        ]
+
+    def rim_all(rim):
+        return pltpu.make_async_remote_copy(
+            src_ref=rim_out.at[rim],
+            dst_ref=rim_in.at[rim],
+            send_sem=rim_send.at[rim],
+            recv_sem=rim_recv.at[rim],
+            device_id=home_of(0, shift_of(rim), 0),
+            device_id_type=MESH,
+        )
+
+    def side_copies(side):
+        return [
+            pltpu.make_async_remote_copy(
+                src_ref=out_buf.at[U, j],
+                dst_ref=side_in.at[side],
+                send_sem=side_send.at[side],
+                recv_sem=side_recv.at[side],
+                device_id=home_of(j, 0, 1 if side == 0 else lons - 1),
+                device_id_type=MESH,
+            )
+            for j in every
+        ]
+
+    def side_all(side):
+        return pltpu.make_async_remote_copy(
+            src_ref=out_buf.at[U],
+            dst_ref=out_buf.at[U],
+            send_sem=side_send.at[side],
+            recv_sem=side_recv.at[side],
+            device_id=home_of(0, 0, 1),
+            device_id_type=MESH,
+        )
+
+    def corner_copies(side, rim):
+        return [
+            pltpu.make_async_remote_copy(
+                src_ref=rim_out.at[rim, j],
+                dst_ref=corner_in.at[side, rim],
+                send_sem=corner_send.at[side, rim],
+                recv_sem=corner_recv.at[side, rim],
+                device_id=home_of(j, shift_of(rim), 1 if side == 0 else lons - 1),
+                device_id_type=MESH,
+            )
+            for j in every
+        ]
+
+    def corner_all(side, rim):
+        return pltpu.make_async_remote_copy(
+            src_ref=rim_out.at[rim],
+            dst_ref=rim_in.at[rim],
+            send_sem=corner_send.at[side, rim],
+            recv_sem=corner_recv.at[side, rim],
+            device_id=home_of(0, shift_of(rim), 1),
+            device_id_type=MESH,
+        )
+
+    def sends_rim(rim):
+        return has_high if rim == 0 else has_low
+
+    def gets_rim(rim):
+        return has_low if rim == 0 else has_high
+
+    def sends_side(side):
+        return me == (peers - 1 if side == 0 else 0)
+
+    def start_rims():
+        for side in range(2):
+
+            @pl.when(sends_side(side))
+            def _():
+                for copy in side_copies(side):
+                    copy.start()
+
+        for rim in range(2):
+
+            @pl.when(sends_rim(rim))
+            def _():
+                for copy in rim_copies(rim):
+                    copy.start()
+
+            for side in range(2):
+
+                @pl.when(jnp.logical_and(sends_side(side), sends_rim(rim)))
+                def _():
+                    for copy in corner_copies(side, rim):
+                        copy.start()
+
+    def wait_rims():
+        for side in range(2):
+            side_copies(side)[0].wait_recv()
+        for rim in range(2):
+
+            @pl.when(gets_rim(rim))
+            def _():
+                rim_all(rim).wait_recv()
+                for side in range(2):
+                    corner_copies(side, rim)[0].wait_recv()
+
+    def wait_rims_sent():
+        for side in range(2):
+
+            @pl.when(sends_side(side))
+            def _():
+                side_all(side).wait_send()
+
+        for rim in range(2):
+
+            @pl.when(sends_rim(rim))
+            def _():
+                rim_all(rim).wait_send()
+
+            for side in range(2):
+
+                @pl.when(jnp.logical_and(sends_side(side), sends_rim(rim)))
+                def _():
+                    corner_all(side, rim).wait_send()
+
+    def rim_pack(rows):
+        half = channels // 2
+        shape = (2 * mem * peers, mem * peers)
+        i, k = iota(shape, 0), iota(shape, 1)
+        same = (i // (2 * mem)) * mem + i % mem == k
+        upper = (i // mem) % 2 == 1
+        low = jnp.where(jnp.logical_and(same, jnp.logical_not(upper)), 1.0, 0.0).astype(BF)
+        high = jnp.where(jnp.logical_and(same, upper), 1.0, 0.0).astype(BF)
+        return nn(low, rows[:, :half]) + nn(high, rows[:, half:])
+
+    def rim_rows(rim):
+        got = rim_in[rim].reshape(2 * mem * peers, channels // 2).astype(BF)
+        shape = (mem * lon, 2 * mem * peers)
+        i, k = iota(shape, 0), iota(shape, 1)
+        row = lax.rem(i % lon - me + peers, peers) * (2 * mem) + i // lon
+        low = jnp.where(k == row, 1.0, 0.0).astype(BF)
+        high = jnp.where(k == row + mem, 1.0, 0.0).astype(BF)
+        return jnp.concatenate([nn(low, got), nn(high, got)], axis=1).astype(BF)
+
+    def side_column(side):
+        half = channels // 2
+        per = mem * lat
+        main = side_in[side].astype(F32)
+        column_ref[side, 0:per, 0:half] = main[:per]
+        column_ref[side, 0:per, half:channels] = main[per:]
+        for rim in range(2):
+            at = per + rim * mem
+            column_ref[side, at : at + mem, 0:half] = corner_in[side, rim, 0:mem]
+            column_ref[side, at : at + mem, half:channels] = corner_in[side, rim, mem : 2 * mem]
+        return column_ref[side].astype(BF)
 
     strip = lat + 2
-    extra = 3 * lon
-
-    def column_source(shift):
-        def source(i):
-            a, b = i // lon, i % lon
-            inner = a * lon + b + shift
-            which = jnp.where(a == 0, 0, jnp.where(a == strip - 1, 2, 1))
-            row = jnp.where(a == 0, lat - 1, jnp.where(a == strip - 1, 0, a - 1))
-            base = (mem * lat if shift < 0 else 0) + row
-            outer = strip * lon + which * lon + base
-            edge = b == (0 if shift < 0 else lon - 1)
-            return jnp.where(edge, outer, inner), edge
-
-        return source
-
-    def shifted(halo, body, m, shift):
-        low = jnp.where(my_lat > 0, halo[m, 0].astype(F32), 0.0).astype(BF)
-        high = jnp.where(my_lat < lats - 1, halo[m, strip - 1].astype(F32), 0.0).astype(BF)
-        middle = body(m)
-        field = jnp.concatenate([low, middle, high], axis=0)
+
+    def cot_edge(m, shift, a):
+        which = jnp.where(a == 0, 0, jnp.where(a == strip - 1, 2, 1))
+        row = jnp.where(a == 0, lat - 1, jnp.where(a == strip - 1, 0, a - 1))
+        return which * lon + (mem * lat if shift < 0 else 0) + m * lat + row
+
+    def up_edge(m, shift, a):
+        outer = mem * lat + m
+        return jnp.where(a == 0, outer, jnp.where(a == strip - 1, outer + mem, m * lat + a - 1))
+
+    def shifted(field, columns, edge_row, m, shift):
         if shift == 0:
             return field
-        side = 0 if shift < 0 else 1
-        columns = halo[side, lat + 2 : lat + 5].reshape(extra, channels)
-        shape = (strip * lon, strip * lon + extra)
-        source, edge = column_source(shift)(iota(shape, 0))
-        source = jnp.where(edge, source + m * lat, source)
-        row = iota(shape, 0) // lon
+        shape = (strip * lon, strip * lon + columns.shape[0])
+        a, b = iota(shape, 0) // lon, iota(shape, 0) % lon
+        outer = strip * lon + edge_row(m, shift, a)
+        source = jnp.where(b == (0 if shift < 0 else lon - 1), outer, a * lon + b + shift)
         open_row = jnp.logical_and(
-            jnp.logical_or(row > 0, my_lat > 0),
-            jnp.logical_or(row < strip - 1, my_lat < lats - 1),
+            jnp.logical_or(a > 0, has_low), jnp.logical_or(a < strip - 1, has_high)
         )
         pick = jnp.where(jnp.logical_and(iota(shape, 1) == source, open_row), 1.0, 0.0).astype(BF)
         return nn(pick, jnp.concatenate([field, columns], axis=0)).astype(BF)
 
-    def conv(halo, body, adjoint):
+    def conv(fields, columns, edge_row, adjoint):
         total = None
         for c in range(3):
             shift = 1 - c if adjoint else c - 1
-            wide = [shifted(halo, body, m, shift) for m in range(mem)]
+            side = 0 if shift < 0 else 1
+            wide = [shifted(fields[m], columns[side], edge_row, m, shift) for m in range(mem)]
             for r in range(3):
                 start = (2 - r if adjoint else r) * lon
                 window = jnp.concatenate([w[start : start + lat * lon] for w in wide], axis=0)
@@ -379,12 +581,24 @@
                 total = term if total is None else total + term
         return total
 
-    def cot_body(m):
-        return cot_ref[m].reshape(lat * lon, channels)
-
-    def up_body(m):
-        return field_ref[m].reshape(lat * lon, channels)
-
+    def closed(rows, there):
+        return jnp.where(there, rows.astype(F32), 0.0).astype(BF)
+
+    @pl.when(jnp.logical_not(has_low))
+    def _():
+        halo_cot[:, 0] = jnp.zeros((mem, lon, channels), BF)
+        halo_cot[:, lat + 2] = jnp.zeros((mem, lon, channels), BF)
+        rim_in[0] = jnp.zeros(rim_in.shape[1:], F32)
+        corner_in[:, 0] = jnp.zeros((2,) + corner_in.shape[2:], F32)
+
+    @pl.when(jnp.logical_not(has_high))
+    def _():
+        halo_cot[:, lat + 1] = jnp.zeros((mem, lon, channels), BF)
+        halo_cot[:, lat + 4] = jnp.zeros((mem, lon, channels), BF)
+        rim_in[1] = jnp.zeros(rim_in.shape[1:], F32)
+        corner_in[:, 1] = jnp.zeros((2,) + corner_in.shape[2:], F32)
+
+    column_ref[...] = jnp.zeros(column_ref.shape, F32)
     loads[0].wait()
     ens = ens_ref[...].reshape(cells, channels)
     loads[1].wait()
@@ -394,22 +608,33 @@
     in_buf[X, 0] = packed[0]
     edge_cot[...] = nn(edges, cot).astype(BF)
     pl.semaphore_wait(barrier, len(close) + len(around))
-    for device in (along(-2), along(2), twin):
-        pl.semaphore_signal(flag.at[0], inc=1, device_id=device, device_id_type=MESH)
-    cot_copies = halo_copies(0, cot_ref, edge_cot, halo_cot)
-    for copy in cot_copies:
-        copy.start()
-    pl.semaphore_wait(flag.at[0], 3)
-    for device in (along(-2), along(2)):
-        pl.semaphore_signal(flag.at[1], inc=1, device_id=device, device_id_type=MESH)
-    pl.semaphore_wait(flag.at[1], 2)
-    for copy in exchange(X, 1):
-        copy.start()
+    pl.semaphore_signal(flag, inc=1, device_id=twin, device_id_type=MESH)
+    start_halo()
+    copies = dict(zip(far_first, exchange(X, 1)))
+    for j in far_first:
+        if j % 2 == 0:
+            copies[j].start()
+    pl.semaphore_wait(flag, 1)
+    for j in far_first:
+        if j % 2 == 1:
+            copies[j].start()
 
     ones = head_blocks(channels, members).astype(BF)
     loads[2].wait()
-    wait_halo(0, cot_copies, halo_cot)
-    grad_field = cot.astype(F32) + conv(halo_cot, cot_body, True)
+    wait_halo()
+    cot_fields = [
+        jnp.concatenate(
+            [
+                closed(halo_cot[m, 0], has_low),
+                cot_ref[m].reshape(lat * lon, channels),
+                closed(halo_cot[m, lat + 1], has_high),
+            ],
+            axis=0,
+        )
+        for m in range(mem)
+    ]
+    cot_columns = [halo_cot[side, lat + 2 : lat + 5].reshape(3 * lon, channels) for side in range(2)]
+    grad_field = cot.astype(F32) + conv(cot_fields, cot_columns, cot_edge, True)
     gf_ref[...] = grad_field
     send(G, home_out, grad_field.astype(BF), 1)
 
@@ -421,19 +646,32 @@
     x = receive(X, cell_in).astype(BF)
     updated, saved = cell_forward(x, gain, w_proj, w_out, ones, members)
     send(U, cell_out, updated, -1)
+    for rim, c in enumerate((lat - 1, 0)):
+        rows = updated[c * members : (c + 1) * members]
+        rim_out[rim] = rim_pack(rows).reshape(rim_out.shape[1:])
+    start_rims()
 
     grads = receive(G, cell_in).astype(BF)
     grad_inputs = cell_backward(grads, saved, gain, w_proj, w_out, ones, members)
     send(B, cell_out, grad_inputs.astype(BF), -1)
 
     field = receive(U, home_in)
-    field_ref[...] = field.astype(BF).reshape(field_ref.shape)
-    edge_up[...] = nn(edges, field.astype(BF)).astype(BF)
-    up_copies = halo_copies(1, field_ref, edge_up, halo_up)
-    for copy in up_copies:
-        copy.start()
-    wait_halo(1, up_copies, halo_up)
-    result = field + conv(halo_up, up_body, False)
+    wait_rims()
+    rows = field.astype(BF)
+    low = closed(rim_rows(0), has_low)
+    high = closed(rim_rows(1), has_high)
+    up_fields = [
+        jnp.concatenate(
+            [
+                low[m * lon : (m + 1) * lon],
+                rows[m * lat * lon : (m + 1) * lat * lon],
+                high[m * lon : (m + 1) * lon],
+            ],
+            axis=0,
+        )
+        for m in range(mem)
+    ]
+    result = field + conv(up_fields, [side_column(0), side_column(1)], up_edge, False)
     result_ref[...] = result.astype(BF).reshape(result_ref.shape)
 
     back = receive(B, home_in)
@@ -441,8 +679,8 @@
 
     for kind in (X, G, U, B):
         exchange_all(kind).wait_send()
-    wait_halo_sent(0, cot_copies, halo_cot)
-    wait_halo_sent(1, up_copies, halo_up)
+    wait_halo_sent()
+    wait_rims_sent()
 
 
 def store_kernel(result_in, grad_in, result_out, grad_out, sem):
@@ -484,17 +722,25 @@
             pltpu.VMEM(chunk, BF),
             pltpu.VMEM(chunk, BF),
             pltpu.VMEM(halo, BF),
-            pltpu.VMEM(halo, BF),
             pltpu.VMEM((2 * mem * lat, channels), BF),
-            pltpu.VMEM((2 * mem * lat, channels), BF),
-            pltpu.VMEM(ensemble.shape, BF),
             pltpu.VMEM((mem * lat * lon, channels), F32),
+            pltpu.VMEM((2, peers, 2 * mem, channels // 2), F32),
+            pltpu.VMEM((2, peers, 2 * mem, channels // 2), F32),
+            pltpu.VMEM((2, 2 * mem * lat, channels // 2), BF),
+            pltpu.VMEM((2, 2, 2 * mem, channels // 2), F32),
+            pltpu.VMEM((2, 16, channels), F32),
             pltpu.SemaphoreType.DMA((6,)),
             pltpu.SemaphoreType.DMA((4,)),
             pltpu.SemaphoreType.DMA((4,)),
-            pltpu.SemaphoreType.DMA((2, 3)),
-            pltpu.SemaphoreType.DMA((2, 3)),
-            pltpu.SemaphoreType.REGULAR((2,)),
+            pltpu.SemaphoreType.DMA((5,)),
+            pltpu.SemaphoreType.DMA((5,)),
+            pltpu.SemaphoreType.DMA((2,)),
+            pltpu.SemaphoreType.DMA((2,)),
+            pltpu.SemaphoreType.DMA((2,)),
+            pltpu.SemaphoreType.DMA((2,)),
+            pltpu.SemaphoreType.DMA((2, 2)),
+            pltpu.SemaphoreType.DMA((2, 2)),
+            pltpu.SemaphoreType.REGULAR,
         ],
         compiler_params=pltpu.CompilerParams(
             collective_id=0, has_side_effects=True, vmem_limit_bytes=LIMIT

time: 32.9 us -> 29.8 us (0.906)
  Pallas kernels: 32.2 us -> 29.1 us
    pallas_call x1, Pallas kernels: 31.5 us -> 28.4 us  [per_device(): pl.pallas_call(functools.partial(kernel, dims), out_shape=(field, field),...]
where the time goes in v5:
time: 29.8 us; the launch traced here: 29.7 us
  Pallas kernels  29.1 us (98%)
  between operations  0.64 us (2%)
    pallas_call x1, Pallas kernels, per_device(): pl.pallas_call(functools.partial(kernel, dims), out_shape=(field, field),...  28.4 us
    pallas_call x1, Pallas kernels, per_device(): pl.pallas_call(store_kernel, out_shape=(field, field), in_specs=[vmem, vm...  0.67 us

profile of v5, /device:TPU:1, one launch (start us, length us, event | category | flops | bytes accessed | tf_op | source)
XLA Modules:
  0.0 29.7 jit_solution(11319075992709384187)
XLA Ops:
  0.6 28.4 %shard_map.77 = (bf16[2,4,16,256]{3,2,1,0:T(8,128)(2,1)S(1)}, bf16[2,4,16,256]{3,2,1,0:T(8,128)(2,1)S(1)}) custom-call(bf16[2,4,16,256]{3,2,1,0:T(8,128)(2,1)} %ens_any.1, f32[1,256]{1,0:T(1,128)} %bitcast.1, bf16[256,768]{1,0:T(8,128)(2,1)} %w_proj_any.1, bf16[256,256]{1,0:T(8,128)(2,1)} %w_out_any.1, bf16[3,3,256,256]{3,2,1,0:T(8,128)(2,1)} %conv_any.1, ...), custom_call_target="tpu_custom_call" | custom-call | tf_op jit(solution)/shard_map/pallas_call | solution.py:710
  29.0 0.7 %shard_map.78 = (bf16[2,4,16,256]{3,2,1,0:T(8,128)(2,1)}, bf16[2,4,16,256]{3,2,1,0:T(8,128)(2,1)}) custom-call(bf16[2,4,16,256]{3,2,1,0:T(8,128)(2,1)S(1)} %get-tuple-element.4.result_in, bf16[2,4,16,256]{3,2,1,0:T(8,128)(2,1)S(1)} %get-tuple-element.5.grad_in), custom_call_target="tpu_custom_call" | custom-call | tf_op jit(solution)/shard_map/pallas_call | solution.py:761

commit v6 on v5

--- a/solution.py
+++ b/solution.py
@@ -70,10 +70,12 @@
     v_bd = [spread(values[s], ones) for s in part]
     scores = jnp.concatenate([nt(queries[s], k) for s, k in zip(part, k_bd)], axis=0)
     expd = jnp.exp(scores * scale)
-    soft = expd / nn(expd.astype(BF), ones)
+    narrow = expd.astype(BF)
+    inv_total = 1.0 / nn(narrow, ones)
+    mixed = jnp.concatenate([nn(narrow[s], v) for s, v in zip(part, v_bd)], axis=0)
+    updated = (inputs + nn((mixed * inv_total).astype(BF), w_out)).astype(BF)
+    soft = expd * inv_total
     rounded = soft.astype(BF)
-    mixed = jnp.concatenate([nn(rounded[s], v) for s, v in zip(part, v_bd)], axis=0).astype(BF)
-    updated = (inputs + nn(mixed, w_out)).astype(BF)
     saved = (inputs, inv, q_raw, k_raw, q_fac, k_fac, q_live, k_live, queries, k_bd, v_bd, soft, rounded)
     return updated, saved
 
@@ -523,14 +525,17 @@
         high = jnp.where(jnp.logical_and(same, upper), 1.0, 0.0).astype(BF)
         return nn(low, rows[:, :half]) + nn(high, rows[:, half:])
 
-    def rim_rows(rim):
-        got = rim_in[rim].reshape(2 * mem * peers, channels // 2).astype(BF)
+    def rim_rows(rim, low, high):
+        got = rim_in[rim].astype(F32).reshape(2 * mem * peers, channels // 2).astype(BF)
+        return jnp.concatenate([nn(low, got), nn(high, got)], axis=1).astype(BF)
+
+    def rim_selection():
         shape = (mem * lon, 2 * mem * peers)
         i, k = iota(shape, 0), iota(shape, 1)
         row = lax.rem(i % lon - me + peers, peers) * (2 * mem) + i // lon
         low = jnp.where(k == row, 1.0, 0.0).astype(BF)
         high = jnp.where(k == row + mem, 1.0, 0.0).astype(BF)
-        return jnp.concatenate([nn(low, got), nn(high, got)], axis=1).astype(BF)
+        return low, high
 
     def side_column(side):
         half = channels // 2
@@ -540,8 +545,9 @@
         column_ref[side, 0:per, half:channels] = main[per:]
         for rim in range(2):
             at = per + rim * mem
-            column_ref[side, at : at + mem, 0:half] = corner_in[side, rim, 0:mem]
-            column_ref[side, at : at + mem, half:channels] = corner_in[side, rim, mem : 2 * mem]
+            corner = corner_in[side, rim].astype(F32)
+            column_ref[side, at : at + mem, 0:half] = corner[:mem]
+            column_ref[side, at : at + mem, half:channels] = corner[mem:]
         return column_ref[side].astype(BF)
 
     strip = lat + 2
@@ -555,25 +561,30 @@
         outer = mem * lat + m
         return jnp.where(a == 0, outer, jnp.where(a == strip - 1, outer + mem, m * lat + a - 1))
 
-    def shifted(field, columns, edge_row, m, shift):
-        if shift == 0:
-            return field
-        shape = (strip * lon, strip * lon + columns.shape[0])
+    def picks_of(edge_row, count):
+        return {(m, shift): pick_of(count, edge_row, m, shift) for m in range(mem) for shift in (-1, 1)}
+
+    def pick_of(count, edge_row, m, shift):
+        shape = (strip * lon, strip * lon + count)
         a, b = iota(shape, 0) // lon, iota(shape, 0) % lon
         outer = strip * lon + edge_row(m, shift, a)
         source = jnp.where(b == (0 if shift < 0 else lon - 1), outer, a * lon + b + shift)
         open_row = jnp.logical_and(
             jnp.logical_or(a > 0, has_low), jnp.logical_or(a < strip - 1, has_high)
         )
-        pick = jnp.where(jnp.logical_and(iota(shape, 1) == source, open_row), 1.0, 0.0).astype(BF)
-        return nn(pick, jnp.concatenate([field, columns], axis=0)).astype(BF)
-
-    def conv(fields, columns, edge_row, adjoint):
+        return jnp.where(jnp.logical_and(iota(shape, 1) == source, open_row), 1.0, 0.0).astype(BF)
+
+    def shifted(field, columns, picks, m, shift):
+        if shift == 0:
+            return field
+        return nn(picks[m, shift], jnp.concatenate([field, columns], axis=0)).astype(BF)
+
+    def conv(fields, columns, picks, adjoint):
         total = None
         for c in range(3):
             shift = 1 - c if adjoint else c - 1
             side = 0 if shift < 0 else 1
-            wide = [shifted(fields[m], columns[side], edge_row, m, shift) for m in range(mem)]
+            wide = [shifted(fields[m], columns[side], picks, m, shift) for m in range(mem)]
             for r in range(3):
                 start = (2 - r if adjoint else r) * lon
                 window = jnp.concatenate([w[start : start + lat * lon] for w in wide], axis=0)
@@ -588,15 +599,15 @@
     def _():
         halo_cot[:, 0] = jnp.zeros((mem, lon, channels), BF)
         halo_cot[:, lat + 2] = jnp.zeros((mem, lon, channels), BF)
-        rim_in[0] = jnp.zeros(rim_in.shape[1:], F32)
-        corner_in[:, 0] = jnp.zeros((2,) + corner_in.shape[2:], F32)
+        rim_in[0] = jnp.zeros(rim_in.shape[1:], BF)
+        corner_in[:, 0] = jnp.zeros((2,) + corner_in.shape[2:], BF)
 
     @pl.when(jnp.logical_not(has_high))
     def _():
         halo_cot[:, lat + 1] = jnp.zeros((mem, lon, channels), BF)
         halo_cot[:, lat + 4] = jnp.zeros((mem, lon, channels), BF)
-        rim_in[1] = jnp.zeros(rim_in.shape[1:], F32)
-        corner_in[:, 1] = jnp.zeros((2,) + corner_in.shape[2:], F32)
+        rim_in[1] = jnp.zeros(rim_in.shape[1:], BF)
+        corner_in[:, 1] = jnp.zeros((2,) + corner_in.shape[2:], BF)
 
     column_ref[...] = jnp.zeros(column_ref.shape, F32)
     loads[0].wait()
@@ -621,6 +632,7 @@
 
     ones = head_blocks(channels, members).astype(BF)
     loads[2].wait()
+    cot_picks = picks_of(cot_edge, 3 * lon)
     wait_halo()
     cot_fields = [
         jnp.concatenate(
@@ -634,7 +646,7 @@
         for m in range(mem)
     ]
     cot_columns = [halo_cot[side, lat + 2 : lat + 5].reshape(3 * lon, channels) for side in range(2)]
-    grad_field = cot.astype(F32) + conv(cot_fields, cot_columns, cot_edge, True)
+    grad_field = cot.astype(F32) + conv(cot_fields, cot_columns, cot_picks, True)
     gf_ref[...] = grad_field
     send(G, home_out, grad_field.astype(BF), 1)
 
@@ -648,18 +660,20 @@
     send(U, cell_out, updated, -1)
     for rim, c in enumerate((lat - 1, 0)):
         rows = updated[c * members : (c + 1) * members]
-        rim_out[rim] = rim_pack(rows).reshape(rim_out.shape[1:])
+        rim_out[rim] = rim_pack(rows).reshape(rim_out.shape[1:]).astype(BF)
     start_rims()
 
     grads = receive(G, cell_in).astype(BF)
     grad_inputs = cell_backward(grads, saved, gain, w_proj, w_out, ones, members)
     send(B, cell_out, grad_inputs.astype(BF), -1)
 
+    up_picks = picks_of(up_edge, column_ref.shape[1])
+    rim_picks = rim_selection()
     field = receive(U, home_in)
     wait_rims()
     rows = field.astype(BF)
-    low = closed(rim_rows(0), has_low)
-    high = closed(rim_rows(1), has_high)
+    low = closed(rim_rows(0, *rim_picks), has_low)
+    high = closed(rim_rows(1, *rim_picks), has_high)
     up_fields = [
         jnp.concatenate(
             [
@@ -671,7 +685,7 @@
         )
         for m in range(mem)
     ]
-    result = field + conv(up_fields, [side_column(0), side_column(1)], up_edge, False)
+    result = field + conv(up_fields, [side_column(0), side_column(1)], up_picks, False)
     result_ref[...] = result.astype(BF).reshape(result_ref.shape)
 
     back = receive(B, home_in)
@@ -724,10 +738,10 @@
             pltpu.VMEM(halo, BF),
             pltpu.VMEM((2 * mem * lat, channels), BF),
             pltpu.VMEM((mem * lat * lon, channels), F32),
-            pltpu.VMEM((2, peers, 2 * mem, channels // 2), F32),
-            pltpu.VMEM((2, peers, 2 * mem, channels // 2), F32),
+            pltpu.VMEM((2, peers, 2 * mem, channels // 2), BF),
+            pltpu.VMEM((2, peers, 2 * mem, channels // 2), BF),
             pltpu.VMEM((2, 2 * mem * lat, channels // 2), BF),
-            pltpu.VMEM((2, 2, 2 * mem, channels // 2), F32),
+            pltpu.VMEM((2, 2, 2 * mem, channels // 2), BF),
             pltpu.VMEM((2, 16, channels), F32),
             pltpu.SemaphoreType.DMA((6,)),
             pltpu.SemaphoreType.DMA((4,)),

time: 29.8 us -> 28.9 us (0.970)
  Pallas kernels: 29.1 us -> 28.1 us
    pallas_call x1, Pallas kernels: 28.4 us -> 27.4 us  [per_device(): pl.pallas_call(functools.partial(kernel, dims), out_shape=(field, field),...]
where the time goes in v6:
time: 28.9 us; the launch traced here: 28.7 us
  Pallas kernels  28.1 us (97%)
  between operations  0.64 us (2%)
    pallas_call x1, Pallas kernels, per_device(): pl.pallas_call(functools.partial(kernel, dims), out_shape=(field, field),...  27.4 us
    pallas_call x1, Pallas kernels, per_device(): pl.pallas_call(store_kernel, out_shape=(field, field), in_specs=[vmem, vm...  0.67 us

profile of v6, /device:TPU:1, one launch (start us, length us, event | category | flops | bytes accessed | tf_op | source)
XLA Modules:
  0.0 28.7 jit_solution(15714728175455565678)
XLA Ops:
  0.6 27.4 %shard_map.77 = (bf16[2,4,16,256]{3,2,1,0:T(8,128)(2,1)S(1)}, bf16[2,4,16,256]{3,2,1,0:T(8,128)(2,1)S(1)}) custom-call(bf16[2,4,16,256]{3,2,1,0:T(8,128)(2,1)} %ens_any.1, f32[1,256]{1,0:T(1,128)} %bitcast.1, bf16[256,768]{1,0:T(8,128)(2,1)} %w_proj_any.1, bf16[256,256]{1,0:T(8,128)(2,1)} %w_out_any.1, bf16[3,3,256,256]{3,2,1,0:T(8,128)(2,1)} %conv_any.1, ...), custom_call_target="tpu_custom_call" | custom-call | tf_op jit(solution)/shard_map/pallas_call | solution.py:724
  28.1 0.7 %shard_map.78 = (bf16[2,4,16,256]{3,2,1,0:T(8,128)(2,1)}, bf16[2,4,16,256]{3,2,1,0:T(8,128)(2,1)}) custom-call(bf16[2,4,16,256]{3,2,1,0:T(8,128)(2,1)S(1)} %get-tuple-element.4.result_in, bf16[2,4,16,256]{3,2,1,0:T(8,128)(2,1)S(1)} %get-tuple-element.5.grad_in), custom_call_target="tpu_custom_call" | custom-call | tf_op jit(solution)/shard_map/pallas_call | solution.py:775

commit v7 on v6

--- a/solution.py
+++ b/solution.py
@@ -168,7 +168,7 @@
     halo_cot,
     edge_cot,
     gf_ref,
-    rim_out,
+    side_out,
     rim_in,
     side_in,
     corner_in,
@@ -218,7 +218,7 @@
 
     around = [(a, b) for a in (-1, 0, 1) for b in (-1, 0, 1) if (a, b) != (0, 0)]
     barrier = pltpu.get_barrier_semaphore()
-    far_first = sorted(range(1, peers), key=lambda j: -min(j, peers - j))
+    far_first = sorted(range(1, peers), key=lambda j: -(min(j, peers - j) // 2 + 2 * (j % 2)))
     ring = peers // 2
     my_z, my_y = me // 2, lax.rem(me, 2)
 
@@ -233,20 +233,26 @@
     for d_lat, d_lon in around:
         pl.semaphore_signal(barrier, inc=1, device_id=near(d_lat, d_lon), device_id_type=MESH)
 
+    blocks = peers // lat
+    width = lon // blocks
+    my_row, my_block = me // blocks, lax.rem(me, blocks)
+
     def home_source(i):
-        j, m, a = i // (mem * lat), (i // lat) % mem, i % lat
-        return (m * lat + a) * lon + lax.rem(me + j, peers)
+        j, m, c = i // (mem * width), (i // width) % mem, i % width
+        q = lax.rem(me + j, peers)
+        return (m * lat + q // blocks) * lon + lax.rem(q, blocks) * width + c
 
     def home_target(i):
         m, a, b = i // (lat * lon), (i // lon) % lat, i % lon
-        return lax.rem(b - me + peers, peers) * (mem * lat) + m * lat + a
+        j = lax.rem(a * blocks + b // width - me + peers, peers)
+        return (j * mem + m) * width + b % width
 
     def cell_source(i):
         c, j, m = i // members, (i // mem) % peers, i % mem
-        return (j * mem + m) * lat + c
+        return (j * mem + m) * width + c
 
     def cell_target(i):
-        j, m, c = i // (mem * lat), (i // lat) % mem, i % lat
+        j, m, c = i // (mem * width), (i // width) % mem, i % width
         return (c * peers + j) * mem + m
 
     def edge_source(i):
@@ -260,7 +266,7 @@
     cell_out = one_hot(square, cell_target)
     edges = one_hot((2 * mem * lat, cells), edge_source)
 
-    def exchange(kind, sign):
+    def exchange(kind, sign, group):
         return [
             pltpu.make_async_remote_copy(
                 src_ref=out_buf.at[kind, j],
@@ -270,7 +276,7 @@
                 device_id=partner(j if sign > 0 else peers - j),
                 device_id_type=MESH,
             )
-            for j in far_first
+            for j in group
         ]
 
     def exchange_all(kind):
@@ -287,7 +293,7 @@
         packed = pack(nn(order, rows), peers)
         out_buf[kind] = packed
         in_buf[kind, 0] = packed[0]
-        for copy in exchange(kind, sign):
+        for copy in exchange(kind, sign, far_first):
             copy.start()
 
     def receive(kind, order):
@@ -373,149 +379,131 @@
             halo_columns(2).wait_send()
             halo_group(-1)[2].wait_send()
 
-    every = [0] + far_first
-
-    def shift_of(rim):
-        return 1 if rim == 0 else lats - 1
-
-    def home_of(j, d_lat, d_lon):
+    far, close_by = far_first[: peers // 2], far_first[peers // 2 :] + [0]
+
+    def home_of(j, rim, side):
         return {
             "member": lax.rem(me + peers - j, peers),
-            "lat": lax.rem(my_lat + d_lat, lats),
-            "lon": lax.rem(my_lon + d_lon, lons),
+            "lat": lax.rem(my_lat + (0 if rim is None else 1 if rim == 0 else lats - 1), lats),
+            "lon": lax.rem(my_lon + (0 if side is None else 1 if side == 0 else lons - 1), lons),
         }
 
-    def rim_copies(rim):
-        return [
-            pltpu.make_async_remote_copy(
-                src_ref=rim_out.at[rim, j],
-                dst_ref=rim_in.at[rim, j],
-                send_sem=rim_send.at[rim],
-                recv_sem=rim_recv.at[rim],
-                device_id=home_of(j, shift_of(rim), 0),
-                device_id_type=MESH,
-            )
-            for j in every
-        ]
-
-    def rim_all(rim):
-        return pltpu.make_async_remote_copy(
-            src_ref=rim_out.at[rim],
-            dst_ref=rim_in.at[rim],
-            send_sem=rim_send.at[rim],
-            recv_sem=rim_recv.at[rim],
-            device_id=home_of(0, shift_of(rim), 0),
-            device_id_type=MESH,
-        )
-
-    def side_copies(side):
+    def rim_copies(rim, group):
         return [
             pltpu.make_async_remote_copy(
                 src_ref=out_buf.at[U, j],
-                dst_ref=side_in.at[side],
+                dst_ref=rim_in.at[rim, my_block],
+                send_sem=rim_send.at[rim],
+                recv_sem=rim_recv.at[rim],
+                device_id=home_of(j, rim, None),
+                device_id_type=MESH,
+            )
+            for j in group
+        ]
+
+    def side_copies(side, group):
+        return [
+            pltpu.make_async_remote_copy(
+                src_ref=side_out.at[side, j],
+                dst_ref=side_in.at[side, my_row],
                 send_sem=side_send.at[side],
                 recv_sem=side_recv.at[side],
-                device_id=home_of(j, 0, 1 if side == 0 else lons - 1),
+                device_id=home_of(j, None, side),
                 device_id_type=MESH,
             )
-            for j in every
+            for j in group
         ]
 
-    def side_all(side):
-        return pltpu.make_async_remote_copy(
-            src_ref=out_buf.at[U],
-            dst_ref=out_buf.at[U],
-            send_sem=side_send.at[side],
-            recv_sem=side_recv.at[side],
-            device_id=home_of(0, 0, 1),
-            device_id_type=MESH,
-        )
-
-    def corner_copies(side, rim):
+    def corner_copies(side, rim, group):
         return [
             pltpu.make_async_remote_copy(
-                src_ref=rim_out.at[rim, j],
+                src_ref=side_out.at[side, j],
                 dst_ref=corner_in.at[side, rim],
                 send_sem=corner_send.at[side, rim],
                 recv_sem=corner_recv.at[side, rim],
-                device_id=home_of(j, shift_of(rim), 1 if side == 0 else lons - 1),
+                device_id=home_of(j, rim, side),
                 device_id_type=MESH,
             )
-            for j in every
+            for j in group
         ]
 
-    def corner_all(side, rim):
+    def bytes_of(ref, send_sem, recv_sem):
         return pltpu.make_async_remote_copy(
-            src_ref=rim_out.at[rim],
-            dst_ref=rim_in.at[rim],
-            send_sem=corner_send.at[side, rim],
-            recv_sem=corner_recv.at[side, rim],
-            device_id=home_of(0, shift_of(rim), 1),
+            src_ref=ref,
+            dst_ref=ref,
+            send_sem=send_sem,
+            recv_sem=recv_sem,
+            device_id=partner(1),
             device_id_type=MESH,
         )
 
-    def sends_rim(rim):
-        return has_high if rim == 0 else has_low
-
     def gets_rim(rim):
         return has_low if rim == 0 else has_high
 
+    def sends_rim(rim):
+        if rim == 0:
+            return jnp.logical_and(has_high, my_row == lat - 1)
+        return jnp.logical_and(has_low, my_row == 0)
+
     def sends_side(side):
-        return me == (peers - 1 if side == 0 else 0)
-
-    def start_rims():
+        return my_block == (blocks - 1 if side == 0 else 0)
+
+    def start_rims(group):
+        for rim in range(2):
+
+            @pl.when(sends_rim(rim))
+            def _():
+                for copy in rim_copies(rim, group):
+                    copy.start()
+
         for side in range(2):
 
             @pl.when(sends_side(side))
             def _():
-                for copy in side_copies(side):
+                for copy in side_copies(side, group):
                     copy.start()
 
+                for rim in range(2):
+
+                    @pl.when(sends_rim(rim))
+                    def _():
+                        for copy in corner_copies(side, rim, group):
+                            copy.start()
+
+    def wait_rims():
+        for side in range(2):
+            bytes_of(side_in.at[side], side_send.at[side], side_recv.at[side]).wait_recv()
+        for rim in range(2):
+
+            @pl.when(gets_rim(rim))
+            def _():
+                bytes_of(rim_in.at[rim], rim_send.at[rim], rim_recv.at[rim]).wait_recv()
+                for side in range(2):
+                    bytes_of(
+                        corner_in.at[side, rim], corner_send.at[side, rim], corner_recv.at[side, rim]
+                    ).wait_recv()
+
+    def wait_rims_sent():
         for rim in range(2):
 
             @pl.when(sends_rim(rim))
             def _():
-                for copy in rim_copies(rim):
-                    copy.start()
-
-            for side in range(2):
-
-                @pl.when(jnp.logical_and(sends_side(side), sends_rim(rim)))
-                def _():
-                    for copy in corner_copies(side, rim):
-                        copy.start()
-
-    def wait_rims():
-        for side in range(2):
-            side_copies(side)[0].wait_recv()
-        for rim in range(2):
-
-            @pl.when(gets_rim(rim))
-            def _():
-                rim_all(rim).wait_recv()
-                for side in range(2):
-                    corner_copies(side, rim)[0].wait_recv()
-
-    def wait_rims_sent():
+                bytes_of(out_buf.at[U], rim_send.at[rim], rim_recv.at[rim]).wait_send()
+
         for side in range(2):
 
             @pl.when(sends_side(side))
             def _():
-                side_all(side).wait_send()
-
-        for rim in range(2):
-
-            @pl.when(sends_rim(rim))
-            def _():
-                rim_all(rim).wait_send()
-
-            for side in range(2):
-
-                @pl.when(jnp.logical_and(sends_side(side), sends_rim(rim)))
-                def _():
-                    corner_all(side, rim).wait_send()
-
-    def rim_pack(rows):
+                bytes_of(side_out.at[side], side_send.at[side], side_recv.at[side]).wait_send()
+                for rim in range(2):
+
+                    @pl.when(sends_rim(rim))
+                    def _():
+                        bytes_of(
+                            side_out.at[side], corner_send.at[side, rim], corner_recv.at[side, rim]
+                        ).wait_send()
+
+    def side_pack(rows):
         half = channels // 2
         shape = (2 * mem * peers, mem * peers)
         i, k = iota(shape, 0), iota(shape, 1)
@@ -525,29 +513,20 @@
         high = jnp.where(jnp.logical_and(same, upper), 1.0, 0.0).astype(BF)
         return nn(low, rows[:, :half]) + nn(high, rows[:, half:])
 
-    def rim_rows(rim, low, high):
-        got = rim_in[rim].astype(F32).reshape(2 * mem * peers, channels // 2).astype(BF)
-        return jnp.concatenate([nn(low, got), nn(high, got)], axis=1).astype(BF)
-
-    def rim_selection():
-        shape = (mem * lon, 2 * mem * peers)
-        i, k = iota(shape, 0), iota(shape, 1)
-        row = lax.rem(i % lon - me + peers, peers) * (2 * mem) + i // lon
-        low = jnp.where(k == row, 1.0, 0.0).astype(BF)
-        high = jnp.where(k == row + mem, 1.0, 0.0).astype(BF)
-        return low, high
+    def rim_source(i):
+        m, b = i // lon, i % lon
+        return ((b // width) * mem + m) * width + b % width
+
+    def rim_rows(rim, pick):
+        return nn(pick, unpack(rim_in[rim])).astype(BF)
 
     def side_column(side):
         half = channels // 2
-        per = mem * lat
-        main = side_in[side].astype(F32)
-        column_ref[side, 0:per, 0:half] = main[:per]
-        column_ref[side, 0:per, half:channels] = main[per:]
-        for rim in range(2):
-            at = per + rim * mem
-            corner = corner_in[side, rim].astype(F32)
-            column_ref[side, at : at + mem, 0:half] = corner[:mem]
-            column_ref[side, at : at + mem, half:channels] = corner[mem:]
+        parts = [side_in.at[side, a] for a in range(lat)] + [corner_in.at[side, rim] for rim in range(2)]
+        for n, part in enumerate(parts):
+            rows = part[...].astype(F32)
+            column_ref[side, n * mem : (n + 1) * mem, 0:half] = rows[:mem]
+            column_ref[side, n * mem : (n + 1) * mem, half:channels] = rows[mem:]
         return column_ref[side].astype(BF)
 
     strip = lat + 2
@@ -558,8 +537,8 @@
         return which * lon + (mem * lat if shift < 0 else 0) + m * lat + row
 
     def up_edge(m, shift, a):
-        outer = mem * lat + m
-        return jnp.where(a == 0, outer, jnp.where(a == strip - 1, outer + mem, m * lat + a - 1))
+        outer = jnp.where(a == 0, lat, jnp.where(a == strip - 1, lat + 1, a - 1))
+        return outer * mem + m
 
     def picks_of(edge_row, count):
         return {(m, shift): pick_of(count, edge_row, m, shift) for m in range(mem) for shift in (-1, 1)}
@@ -621,7 +600,7 @@
     pl.semaphore_wait(barrier, len(close) + len(around))
     pl.semaphore_signal(flag, inc=1, device_id=twin, device_id_type=MESH)
     start_halo()
-    copies = dict(zip(far_first, exchange(X, 1)))
+    copies = dict(zip(far_first, exchange(X, 1, far_first)))
     for j in far_first:
         if j % 2 == 0:
             copies[j].start()
@@ -657,23 +636,28 @@
     w_out = w_out_ref[...]
     x = receive(X, cell_in).astype(BF)
     updated, saved = cell_forward(x, gain, w_proj, w_out, ones, members)
-    send(U, cell_out, updated, -1)
-    for rim, c in enumerate((lat - 1, 0)):
+    packed = pack(nn(cell_out, updated), peers)
+    out_buf[U] = packed
+    in_buf[U, 0] = packed[0]
+    for side, c in enumerate((width - 1, 0)):
         rows = updated[c * members : (c + 1) * members]
-        rim_out[rim] = rim_pack(rows).reshape(rim_out.shape[1:]).astype(BF)
-    start_rims()
+        side_out[side] = side_pack(rows).reshape(side_out.shape[1:]).astype(BF)
+    for group in (far, close_by):
+        for copy in exchange(U, -1, [j for j in group if j]):
+            copy.start()
+        start_rims(group)
 
     grads = receive(G, cell_in).astype(BF)
     grad_inputs = cell_backward(grads, saved, gain, w_proj, w_out, ones, members)
     send(B, cell_out, grad_inputs.astype(BF), -1)
 
     up_picks = picks_of(up_edge, column_ref.shape[1])
-    rim_picks = rim_selection()
+    rim_pick = one_hot((mem * lon, mem * lon), rim_source)
     field = receive(U, home_in)
     wait_rims()
     rows = field.astype(BF)
-    low = closed(rim_rows(0, *rim_picks), has_low)
-    high = closed(rim_rows(1, *rim_picks), has_high)
+    low = closed(rim_rows(0, rim_pick), has_low)
+    high = closed(rim_rows(1, rim_pick), has_high)
     up_fields = [
         jnp.concatenate(
             [
@@ -739,8 +723,8 @@
             pltpu.VMEM((2 * mem * lat, channels), BF),
             pltpu.VMEM((mem * lat * lon, channels), F32),
             pltpu.VMEM((2, peers, 2 * mem, channels // 2), BF),
-            pltpu.VMEM((2, peers, 2 * mem, channels // 2), BF),
-            pltpu.VMEM((2, 2 * mem * lat, channels // 2), BF),
+            pltpu.VMEM((2, peers // lat) + chunk[2:], BF),
+            pltpu.VMEM((2, lat, 2 * mem, channels // 2), BF),
             pltpu.VMEM((2, 2, 2 * mem, channels // 2), BF),
             pltpu.VMEM((2, 16, channels), F32),
             pltpu.SemaphoreType.DMA((6,)),

time: 28.9 us -> 27.7 us (0.958)
  Pallas kernels: 28.1 us -> 26.9 us
    pallas_call x1, Pallas kernels: 27.4 us -> 26.2 us  [per_device(): pl.pallas_call(functools.partial(kernel, dims), out_shape=(field, field),...]
where the time goes in v7:
time: 27.7 us; the launch traced here: 27.6 us
  Pallas kernels  26.9 us (97%)
  between operations  0.64 us (2%)
    pallas_call x1, Pallas kernels, per_device(): pl.pallas_call(functools.partial(kernel, dims), out_shape=(field, field),...  26.2 us
    pallas_call x1, Pallas kernels, per_device(): pl.pallas_call(store_kernel, out_shape=(field, field), in_specs=[vmem, vm...  0.67 us

profile of v7, /device:TPU:1, one launch (start us, length us, event | category | flops | bytes accessed | tf_op | source)
XLA Modules:
  0.0 27.6 jit_solution(8229688647474086628)
XLA Ops:
  0.6 26.2 %shard_map.77 = (bf16[2,4,16,256]{3,2,1,0:T(8,128)(2,1)S(1)}, bf16[2,4,16,256]{3,2,1,0:T(8,128)(2,1)S(1)}) custom-call(bf16[2,4,16,256]{3,2,1,0:T(8,128)(2,1)} %ens_any.1, f32[1,256]{1,0:T(1,128)} %bitcast.1, bf16[256,768]{1,0:T(8,128)(2,1)} %w_proj_any.1, bf16[256,256]{1,0:T(8,128)(2,1)} %w_out_any.1, bf16[3,3,256,256]{3,2,1,0:T(8,128)(2,1)} %conv_any.1, ...), custom_call_target="tpu_custom_call" | custom-call | tf_op jit(solution)/shard_map/pallas_call | solution.py:708
  26.9 0.7 %shard_map.78 = (bf16[2,4,16,256]{3,2,1,0:T(8,128)(2,1)}, bf16[2,4,16,256]{3,2,1,0:T(8,128)(2,1)}) custom-call(bf16[2,4,16,256]{3,2,1,0:T(8,128)(2,1)S(1)} %get-tuple-element.4.result_in, bf16[2,4,16,256]{3,2,1,0:T(8,128)(2,1)S(1)} %get-tuple-element.5.grad_in), custom_call_target="tpu_custom_call" | custom-call | tf_op jit(solution)/shard_map/pallas_call | solution.py:759

commit v8 on v7

--- a/solution.py
+++ b/solution.py
@@ -204,9 +204,6 @@
     loads = [
         pltpu.make_async_copy(src, dst, load_sem.at[i]) for i, (src, dst) in enumerate(pairs)
     ]
-    for load in loads:
-        load.start()
-
     def partner(j):
         return {"member": lax.rem(me + j, peers)}
 
@@ -232,6 +229,9 @@
         pl.semaphore_signal(barrier, inc=1, device_id=device, device_id_type=MESH)
     for d_lat, d_lon in around:
         pl.semaphore_signal(barrier, inc=1, device_id=near(d_lat, d_lon), device_id_type=MESH)
+
+    for load in loads:
+        load.start()
 
     blocks = peers // lat
     width = lon // blocks
@@ -599,11 +599,11 @@
     edge_cot[...] = nn(edges, cot).astype(BF)
     pl.semaphore_wait(barrier, len(close) + len(around))
     pl.semaphore_signal(flag, inc=1, device_id=twin, device_id_type=MESH)
-    start_halo()
     copies = dict(zip(far_first, exchange(X, 1, far_first)))
     for j in far_first:
         if j % 2 == 0:
             copies[j].start()
+    start_halo()
     pl.semaphore_wait(flag, 1)
     for j in far_first:
         if j % 2 == 1:

time: 27.7 us -> 27.6 us (level)
  no operation moved by 1% of the time
where the time goes in v8:
time: 27.6 us
  Pallas kernels  26.9 us (97%)
  between operations  0.64 us (2%)
    pallas_call x1, Pallas kernels, per_device(): pl.pallas_call(functools.partial(kernel, dims), out_shape=(field, field),...  26.2 us
    pallas_call x1, Pallas kernels, per_device(): pl.pallas_call(store_kernel, out_shape=(field, field), in_specs=[vmem, vm...  0.67 us

profile of v8, /device:TPU:1, one launch (start us, length us, event | category | flops | bytes accessed | tf_op | source)
XLA Modules:
  0.0 27.6 jit_solution(13768621581438028052)
XLA Ops:
  0.6 26.2 %shard_map.77 = (bf16[2,4,16,256]{3,2,1,0:T(8,128)(2,1)S(1)}, bf16[2,4,16,256]{3,2,1,0:T(8,128)(2,1)S(1)}) custom-call(bf16[2,4,16,256]{3,2,1,0:T(8,128)(2,1)} %ens_any.1, f32[1,256]{1,0:T(1,128)} %bitcast.1, bf16[256,768]{1,0:T(8,128)(2,1)} %w_proj_any.1, bf16[256,256]{1,0:T(8,128)(2,1)} %w_out_any.1, bf16[3,3,256,256]{3,2,1,0:T(8,128)(2,1)} %conv_any.1, ...), custom_call_target="tpu_custom_call" | custom-call | tf_op jit(solution)/shard_map/pallas_call | solution.py:708
  26.9 0.7 %shard_map.78 = (bf16[2,4,16,256]{3,2,1,0:T(8,128)(2,1)}, bf16[2,4,16,256]{3,2,1,0:T(8,128)(2,1)}) custom-call(bf16[2,4,16,256]{3,2,1,0:T(8,128)(2,1)S(1)} %get-tuple-element.4.result_in, bf16[2,4,16,256]{3,2,1,0:T(8,128)(2,1)S(1)} %get-tuple-element.5.grad_in), custom_call_target="tpu_custom_call" | custom-call | tf_op jit(solution)/shard_map/pallas_call | solution.py:759

commit v9 on v7

--- a/solution.py
+++ b/solution.py
@@ -57,10 +57,9 @@
     inputs = x.astype(F32)
     inv = lax.rsqrt(jnp.mean(inputs * inputs, axis=-1, keepdims=True) + EPSILON)
     normed = (inputs * inv * gain).astype(BF)
-    proj = nn(normed, w_proj).astype(BF)
-    q_raw = proj[:, :channels].astype(F32)
-    k_raw = proj[:, channels : 2 * channels].astype(F32)
-    values = proj[:, 2 * channels :]
+    k_raw = nn(normed, w_proj[:, channels : 2 * channels]).astype(BF).astype(F32)
+    q_raw = nn(normed, w_proj[:, :channels]).astype(BF).astype(F32)
+    values = nn(normed, w_proj[:, 2 * channels :]).astype(BF)
     q_fac, q_live = head_scale(q_raw, ones)
     k_fac, k_live = head_scale(k_raw, ones)
     queries = (q_raw * q_fac).astype(BF)
@@ -559,17 +558,27 @@
         return nn(picks[m, shift], jnp.concatenate([field, columns], axis=0)).astype(BF)
 
     def conv(fields, columns, picks, adjoint):
-        total = None
+        halves = []
+        wide = {}
         for c in range(3):
             shift = 1 - c if adjoint else c - 1
             side = 0 if shift < 0 else 1
-            wide = [shifted(fields[m], columns[side], picks, m, shift) for m in range(mem)]
-            for r in range(3):
-                start = (2 - r if adjoint else r) * lon
-                window = jnp.concatenate([w[start : start + lat * lon] for w in wide], axis=0)
-                term = nt(window, conv_ref[r, c]) if adjoint else nn(window, conv_ref[r, c])
-                total = term if total is None else total + term
-        return total
+            wide[c] = [shifted(fields[m], columns[side], picks, m, shift) for m in range(mem)]
+        count = channels // 2 if adjoint else channels
+        for at in range(0, channels, count):
+            part = pl.ds(at, count)
+            total = None
+            for c in range(3):
+                for r in range(3):
+                    start = (2 - r if adjoint else r) * lon
+                    window = jnp.concatenate([w[start : start + lat * lon] for w in wide[c]], axis=0)
+                    if adjoint:
+                        term = nt(window, conv_ref[r, c, part, :])
+                    else:
+                        term = nn(window, conv_ref[r, c, :, part])
+                    total = term if total is None else total + term
+            halves.append(total)
+        return jnp.concatenate(halves, axis=1) if adjoint else halves[0]
 
     def closed(rows, there):
         return jnp.where(there, rows.astype(F32), 0.0).astype(BF)

time: 27.7 us -> 27.5 us (level)
  Pallas kernels: 26.9 us -> 26.5 us
    pallas_call x1, Pallas kernels: 26.2 us -> 25.9 us  [per_device(): pl.pallas_call(functools.partial(kernel, dims), out_shape=(field, field),...]
where the time goes in v9:
time: 27.5 us; the launch traced here: 27.2 us
  Pallas kernels  26.5 us (96%)
  between operations  0.64 us (2%)
    pallas_call x1, Pallas kernels, per_device(): pl.pallas_call(functools.partial(kernel, dims), out_shape=(field, field),...  25.9 us
    pallas_call x1, Pallas kernels, per_device(): pl.pallas_call(store_kernel, out_shape=(field, field), in_specs=[vmem, vm...  0.67 us

profile of v9, /device:TPU:1, one launch (start us, length us, event | category | flops | bytes accessed | tf_op | source)
XLA Modules:
  0.0 27.2 jit_solution(18091399662183432209)
XLA Ops:
  0.6 25.9 %shard_map.77 = (bf16[2,4,16,256]{3,2,1,0:T(8,128)(2,1)S(1)}, bf16[2,4,16,256]{3,2,1,0:T(8,128)(2,1)S(1)}) custom-call(bf16[2,4,16,256]{3,2,1,0:T(8,128)(2,1)} %ens_any.1, f32[1,256]{1,0:T(1,128)} %bitcast.1, bf16[256,768]{1,0:T(8,128)(2,1)} %w_proj_any.1, bf16[256,256]{1,0:T(8,128)(2,1)} %w_out_any.1, bf16[3,3,256,256]{3,2,1,0:T(8,128)(2,1)} %conv_any.1, ...), custom_call_target="tpu_custom_call" | custom-call | tf_op jit(solution)/shard_map/pallas_call | solution.py:717
  26.5 0.7 %shard_map.78 = (bf16[2,4,16,256]{3,2,1,0:T(8,128)(2,1)}, bf16[2,4,16,256]{3,2,1,0:T(8,128)(2,1)}) custom-call(bf16[2,4,16,256]{3,2,1,0:T(8,128)(2,1)S(1)} %get-tuple-element.4.result_in, bf16[2,4,16,256]{3,2,1,0:T(8,128)(2,1)S(1)} %get-tuple-element.5.grad_in), custom_call_target="tpu_custom_call" | custom-call | tf_op jit(solution)/shard_map/pallas_call | solution.py:768

commit v10 on v9

--- a/solution.py
+++ b/solution.py
@@ -564,9 +564,8 @@
             shift = 1 - c if adjoint else c - 1
             side = 0 if shift < 0 else 1
             wide[c] = [shifted(fields[m], columns[side], picks, m, shift) for m in range(mem)]
-        count = channels // 2 if adjoint else channels
-        for at in range(0, channels, count):
-            part = pl.ds(at, count)
+        for at in range(0, channels, channels // 2):
+            part = pl.ds(at, channels // 2)
             total = None
             for c in range(3):
                 for r in range(3):
@@ -578,7 +577,7 @@
                         term = nn(window, conv_ref[r, c, :, part])
                     total = term if total is None else total + term
             halves.append(total)
-        return jnp.concatenate(halves, axis=1) if adjoint else halves[0]
+        return jnp.concatenate(halves, axis=1)
 
     def closed(rows, there):
         return jnp.where(there, rows.astype(F32), 0.0).astype(BF)

time: 27.5 us -> 27.5 us (level)
  no operation moved by 1% of the time
where the time goes in v10:
time: 27.5 us; the launch traced here: 27.2 us
  Pallas kernels  26.5 us (96%)
  between operations  0.64 us (2%)
    pallas_call x1, Pallas kernels, per_device(): pl.pallas_call(functools.partial(kernel, dims), out_shape=(field, field),...  25.8 us
    pallas_call x1, Pallas kernels, per_device(): pl.pallas_call(store_kernel, out_shape=(field, field), in_specs=[vmem, vm...  0.67 us

profile of v10, /device:TPU:1, one launch (start us, length us, event | category | flops | bytes accessed | tf_op | source)
XLA Modules:
  0.0 27.2 jit_solution(2091652931938757621)
XLA Ops:
  0.6 25.8 %shard_map.77 = (bf16[2,4,16,256]{3,2,1,0:T(8,128)(2,1)S(1)}, bf16[2,4,16,256]{3,2,1,0:T(8,128)(2,1)S(1)}) custom-call(bf16[2,4,16,256]{3,2,1,0:T(8,128)(2,1)} %ens_any.1, f32[1,256]{1,0:T(1,128)} %bitcast.1, bf16[256,768]{1,0:T(8,128)(2,1)} %w_proj_any.1, bf16[256,256]{1,0:T(8,128)(2,1)} %w_out_any.1, bf16[3,3,256,256]{3,2,1,0:T(8,128)(2,1)} %conv_any.1, ...), custom_call_target="tpu_custom_call" | custom-call | tf_op jit(solution)/shard_map/pallas_call | solution.py:716
  26.5 0.7 %shard_map.78 = (bf16[2,4,16,256]{3,2,1,0:T(8,128)(2,1)}, bf16[2,4,16,256]{3,2,1,0:T(8,128)(2,1)}) custom-call(bf16[2,4,16,256]{3,2,1,0:T(8,128)(2,1)S(1)} %get-tuple-element.4.result_in, bf16[2,4,16,256]{3,2,1,0:T(8,128)(2,1)S(1)} %get-tuple-element.5.grad_in), custom_call_target="tpu_custom_call" | custom-call | tf_op jit(solution)/shard_map/pallas_call | solution.py:767
